TPU v7x, 256 devices: a whole 4x4x8 slice. The times are simulated.
256 devices in a mesh: ctx: 4 (over y), row: 4 (over x_hi, core), col: 16 (over x_lo, z).
Axes of the slice: x: 4 (x_hi: 2, x_lo: 2; x = x_hi * 2 + x_lo), y: 4, z: 8, core: 2. Of those that a mesh axis runs over, the one named last changes fastest.
Arguments:
- events: bfloat16 [8192, 4096], P(('ctx', 'row'), 'col'), may hold values from -120 to 120
- domain_ids: int32 [8192], P(('ctx', 'row')), may hold values from 0 to 3
- block_order: int32 [4], replicated, may hold values from 0 to 3, each once
- query_weight: bfloat16 [4096, 4096], P('row', 'col'), may hold values from -0.09375 to 0.09375
- keyval_weight: bfloat16 [4096, 8, 2, 128], P('row'), may hold values from -0.09375 to 0.09375
- head_bias: float32 [32], P('col'), may hold values from -1.5 to 1.5
- out_weight: bfloat16 [4096, 4096], P('row', 'col'), may hold values from -0.09375 to 0.09375
Outputs:
- mixed: bfloat16 [8192, 4096], P(('ctx', 'row'), 'col')
Inputs may be any that keep to these rules, and one draw needn't show every extreme that they name: `block_order`: each index of ctx holds 2048 consecutive events of one block; every place 0 to 3 is named once.
All inputs are finite; a program needn't handle non-finite values.
Results may differ from a plain program's by a relative error of at most 0.0075.
Values may be sent and summed in bfloat16 or wider, within the bound.
No kernel may reach another device: no remote copies, remote signals or barrier semaphores. Data moves between devices by JAX's collectives and lax.ppermute only.
A program may use at most 128 MiB of HBM per device.

v0:
```python
import functools
import math

import jax
import jax.numpy as jnp
from jax import lax
from jax.experimental import pallas as pl
from jax.experimental.pallas import tpu as pltpu
from jax.sharding import Mesh
from jax.sharding import PartitionSpec as P


HD = 128
D = 4096
NZ = 8
NY = 4
norm_eps = 1e-06
BF = jnp.bfloat16
F32 = jnp.float32

SWAP = [(0, 1), (1, 0)]
TAKE_0 = [(xl * 2 + xh, xh * 2 + xl) for xh in range(2) for xl in range(2)]
TAKE_1 = [(xl * 2 + 1 - xh, xh * 2 + xl) for xh in range(2) for xl in range(2)]


def shift(x, axis, size, by):
    return lax.ppermute(x, axis, [(i, (i + by) % size) for i in range(size)])


def ring(x):
    got = {0: x}
    up = down = x
    for s in range(1, 4):
        up = got[s] = shift(up, "z", NZ, 1)
        down = got[NZ - s] = shift(down, "z", NZ, -1)
    pairs = [(c * NZ + i, c * NZ + (i + 1 - 2 * c) % NZ) for c in range(2) for i in range(NZ)]
    last = jnp.where(lax.axis_index("core") == 0, up, down)
    return [got[s] for s in range(NZ) if s != 4], lax.ppermute(last, ("core", "z"), pairs)


def proj_kernel(mode, with_squares, n_w, pick, scal, *refs):
    n_x = {"all": 8, "most": 7, "last": 1}[mode]
    xs, refs = refs[:n_x], refs[n_x:]
    n_ws = 4 if mode == "all" else 2 * n_w
    ws, refs = refs[:n_ws], refs[n_ws:]
    z, core = scal[0], scal[1]
    ones = jnp.ones((8, 256), BF)
    dims = (((1,), (1,)), ((), ()))

    def squares_of(x):
        wide = x.astype(F32)
        sq = wide * wide
        hi = sq.astype(BF)
        lo = (sq - hi.astype(F32)).astype(BF)
        return lax.dot_general(ones, hi, dims, preferred_element_type=F32) + lax.dot_general(
            ones, lo, dims, preferred_element_type=F32
        )

    def column(s):
        return pl.multiple_of(lax.rem(z - s + NZ, NZ) * 256, 256)

    def write(acc, keep, send):
        half = acc.shape[1] // 2

        def put(first):
            mine, other = slice(0, half), slice(half, 2 * half)
            if not first:
                mine, other = other, mine
            keep[...] = acc[:, mine]
            send[: keep.shape[0], :] = acc[:, other].astype(BF)

        flag = scal[pick]
        pl.when(flag == 0)(functools.partial(put, True))
        pl.when(flag != 0)(functools.partial(put, False))

    if mode == "last":
        if with_squares:
            sums, old_sq, keep, send, new_sq, rows_scr, acc = refs
        else:
            sums, keep, send, acc = refs
        off = column(4)
        here = off // 1024 == core
        off = pl.multiple_of(lax.rem(off, 1024), 256)
        x = xs[0][...]

        def add(which):
            width = acc.shape[1] // n_w
            for k in range(n_w):
                cols = slice(k * width, (k + 1) * width)
                acc[:, cols] = sums[:, cols] + jnp.dot(
                    x, ws[2 * k + which][pl.ds(off, 256), :], preferred_element_type=F32
                )

        pl.when(here)(functools.partial(add, 0))
        pl.when(jnp.logical_not(here))(functools.partial(add, 1))
        write(acc, keep, send)
        if with_squares:
            rest = old_sq[...] + squares_of(x)
            new_sq[...] = rest
            rows_scr[...] = jnp.zeros_like(rows_scr)
            for t in range(3):
                term = rest.astype(BF).astype(F32)
                for k in range(4):
                    rows_scr[pl.ds(4 * t + k, 1), :] = term[:1, k * HD : (k + 1) * HD]
                rest = rest - term
            send[keep.shape[0] :, :] = rows_scr[...].astype(BF)
        return

    x_scr = refs[-1]
    order = [s for s in range(NZ) if s != 4]
    for s, ref in zip(order, xs):
        x_scr[:, pl.ds(column(s), 256)] = ref[...]
    if mode == "all":
        x_scr[:, pl.ds(column(4), 256)] = xs[7][...]
        keep, send, acc = refs[0], refs[1], refs[-2]
        half = scal[14]
        acc[...] = sum(
            jnp.dot(
                x_scr[:, pl.ds(pl.multiple_of(c * 1024 + h * 512, 512), 512)],
                w[...],
                preferred_element_type=F32,
            )
            for w, c, h in zip(
                ws, (core, core, 1 - core, 1 - core), (half, 1 - half, half, 1 - half)
            )
        )
        write(acc, keep, send)
        return
    x_scr[:, pl.ds(column(4), 256)] = jnp.zeros((x_scr.shape[0], 256), BF)
    acc = refs[0]
    near = pl.multiple_of(core * 1024, 1024)
    far = pl.multiple_of((1 - core) * 1024, 1024)
    width = acc.shape[1] // n_w
    for k in range(n_w):
        acc[:, k * width : (k + 1) * width] = jnp.dot(
            x_scr[:, pl.ds(near, 1024)], ws[2 * k][...], preferred_element_type=F32
        ) + jnp.dot(x_scr[:, pl.ds(far, 1024)], ws[2 * k + 1][...], preferred_element_type=F32)
    if with_squares:
        refs[1][...] = sum(squares_of(ref[...]) for ref in xs)


VM = pl.BlockSpec(memory_space=pltpu.VMEM)
SM = pl.BlockSpec(memory_space=pltpu.SMEM)


def project_most(scal, xs, ws, with_squares):
    rows = xs[0].shape[0]
    n_w = len(ws) // 2
    total = n_w * ws[0].shape[1]
    out = [jax.ShapeDtypeStruct((rows, total), F32)]
    if with_squares:
        out.append(jax.ShapeDtypeStruct((8, rows), F32))
    return pl.pallas_call(
        functools.partial(proj_kernel, "most", with_squares, n_w, None),
        out_shape=out,
        in_specs=[SM] + [VM] * (len(xs) + len(ws)),
        out_specs=[VM] * len(out),
        scratch_shapes=[pltpu.VMEM((rows, 8 * 256), BF)],
        cost_estimate=pl.CostEstimate(
            flops=2 * rows * 1792 * total, transcendentals=0, bytes_accessed=8 * rows * total
        ),
        compiler_params=pltpu.CompilerParams(vmem_limit_bytes=PROJECT_VMEM),
        name="project_most",
    )(scal, *xs, *ws)


def project_last(scal, pick, last, ws, sums):
    rows = last.shape[0]
    n_w = len(ws) // 2
    total = n_w * ws[0].shape[1]
    squares = len(sums) > 1
    out = [
        jax.ShapeDtypeStruct((rows, total // 2), F32),
        jax.ShapeDtypeStruct((rows + 16 if squares else rows, total // 2), BF),
    ]
    scratch = [pltpu.VMEM((rows, total), F32)]
    if squares:
        out.append(jax.ShapeDtypeStruct((8, rows), F32))
        scratch.insert(0, pltpu.VMEM((16, HD), F32))
    return pl.pallas_call(
        functools.partial(proj_kernel, "last", squares, n_w, pick),
        out_shape=out,
        in_specs=[SM] + [VM] * (1 + len(ws) + len(sums)),
        out_specs=[VM] * len(out),
        scratch_shapes=scratch,
        compiler_params=pltpu.CompilerParams(vmem_limit_bytes=PROJECT_VMEM),
        name="project_last",
    )(scal, last, *ws, *sums)


def project_all(scal, pick, xs, last, ws):
    rows = last.shape[0]
    total = ws[0].shape[1]
    out = [
        jax.ShapeDtypeStruct((rows, total // 2), F32),
        jax.ShapeDtypeStruct((rows, total // 2), BF),
    ]
    return pl.pallas_call(
        functools.partial(proj_kernel, "all", False, 1, pick),
        out_shape=out,
        in_specs=[SM] + [VM] * (8 + len(ws)),
        out_specs=[VM] * len(out),
        scratch_shapes=[pltpu.VMEM((rows, total), F32), pltpu.VMEM((rows, 8 * 256), BF)],
        cost_estimate=pl.CostEstimate(
            flops=2 * rows * 2048 * total, transcendentals=0, bytes_accessed=8 * rows * total
        ),
        compiler_params=pltpu.CompilerParams(vmem_limit_bytes=PROJECT_VMEM),
        name="project_all",
    )(scal, *xs, last, *ws)


PROJECT_VMEM = 20 << 20
ATTEND_VMEM = 28 << 20


def attend_kernel(which, first, final, scal, coef_ref, q_ref, q_other_ref, *refs):
    n = len(which)
    kvs, refs = refs[:n], refs[n:]
    if not first:
        before, refs = refs[0], refs[1:]
    if final:
        own_out, other_out, k_scr, v_scr, q_scr, acc = refs
    else:
        acc, k_scr, v_scr, q_scr = refs
    rows = acc.shape[1]

    def one_hot(ref, at):
        ids = ref[rows:, :].astype(F32)[at // 256 : at // 256 + 1, :]
        lane = lax.broadcasted_iota(jnp.int32, (16, 256), 0)
        hot = (ids == (lane % 4).astype(F32)) & (lane < 8)
        unit = lax.broadcasted_iota(jnp.int32, (16, HD), 0) == lax.broadcasted_iota(
            jnp.int32, (16, HD), 1
        )
        return lax.dot_general(
            hot.astype(F32).astype(BF),
            unit.astype(F32).astype(BF),
            (((0,), (0,)), ((), ())),
            preferred_element_type=F32,
        )

    for i in range(n):
        k_scr[i, :, :HD] = kvs[i][:rows, :HD]
        for at in range(0, rows, 256):
            k_scr[i, at : at + 256, HD:] = one_hot(kvs[i], at).astype(BF)
        v_scr[i] = kvs[i][:rows, HD:]
    for g, ref in enumerate((q_ref, q_other_ref)):
        for at in range(0, rows, 256):
            hot = one_hot(ref, at)
            for h in range(2):
                q_scr[g, h, at : at + 256, HD:] = (hot * coef_ref[h : h + 1, :]).astype(BF)
        for h in range(2):
            q_scr[g, h, :, :HD] = ref[:rows, h * HD : (h + 1) * HD]
    if first:
        acc[...] = jnp.zeros_like(acc)
    else:
        acc[...] = before[...]

    def tile(g, i, ahead=None):
        keys = k_scr[i]
        values = v_scr[i]
        for h in range(2):
            u = lax.dot_general(
                q_scr[g, h], keys, (((1,), (1,)), ((), ())), preferred_element_type=F32
            )
            w = u + u * jnp.tanh(u)
            if ahead is not None:
                t_at = lax.broadcasted_iota(jnp.int32, w.shape, 0)
                u_at = lax.broadcasted_iota(jnp.int32, w.shape, 1)
                w = jnp.where(u_at - t_at <= ahead, w, 0.0)
            acc[g, :, h * HD : (h + 1) * HD] += jnp.dot(
                w.astype(BF), values, preferred_element_type=F32
            )

    def place_of(i):
        at = scal[6 + which[0]]
        for m in range(1, n):
            at = jnp.where(i == m, scal[6 + which[m]], at)
        return at

    if first:

        def one(k, carry):
            g, i = k // n, lax.rem(k, n)
            own = k == 0

            @pl.when(jnp.logical_or(own, place_of(i) < scal[4 + g]))
            def _():
                tile(g, i, jnp.where(own, 0, rows))

            return carry

        lax.fori_loop(0, 2 * n, one, 0)
    else:

        def both(i, carry):
            @pl.when(place_of(i) < scal[4])
            def _():
                tile(0, i)
                tile(1, i)

            return carry

        lax.fori_loop(0, n, both, 0)
    if final:
        own_out[...] = acc[0]
        other_out[...] = acc[1].astype(BF)


def attend(scal, coef, q, q_other, kvs, which, before=None, final=False):
    rows = q.shape[0] - 16
    n = len(kvs)
    sums = jax.ShapeDtypeStruct((2, rows, 2 * HD), F32)
    out = [sums]
    scratch = [
        pltpu.VMEM((n, rows, 2 * HD), BF),
        pltpu.VMEM((n, rows, HD), BF),
        pltpu.VMEM((2, 2, rows, 2 * HD), BF),
    ]
    if final:
        out = [
            jax.ShapeDtypeStruct((rows, 2 * HD), F32),
            jax.ShapeDtypeStruct((rows, 2 * HD), BF),
        ]
        scratch.append(pltpu.VMEM((2, rows, 2 * HD), F32))
    extra = [] if before is None else [before]
    return pl.pallas_call(
        functools.partial(attend_kernel, which, before is None, final),
        out_shape=out,
        in_specs=[SM] + [VM] * (3 + n + len(extra)),
        out_specs=[VM] * len(out),
        scratch_shapes=scratch,
        cost_estimate=pl.CostEstimate(
            flops=n * 2 * 4 * 2 * rows * rows * 256, transcendentals=0, bytes_accessed=1 << 20
        ),
        compiler_params=pltpu.CompilerParams(vmem_limit_bytes=ATTEND_VMEM),
        name="attend",
    )(scal, coef, q, q_other, *kvs, *extra)


def shards(events, domain_ids, block_order, query_weight, keyval_weight, head_bias, out_weight):
    rows = events.shape[0]
    y, xh, core = lax.axis_index("y"), lax.axis_index("xh"), lax.axis_index("core")
    xl, z = lax.axis_index("xl"), lax.axis_index("z")
    chip_x = ("xh", "xl")

    xs, last = ring(events)
    pairs = [
        lax.dynamic_slice(
            keyval_weight, (0, z // 2 + 4 * b, z % 2, 0), (keyval_weight.shape[0], 1, 1, HD)
        ).reshape(-1, HD)
        for b in range(2)
    ]
    kvw = lax.ppermute(jnp.concatenate(pairs, axis=1), chip_x, TAKE_0)
    half = query_weight.shape[0] // 2
    qw_in = lax.dynamic_slice_in_dim(query_weight, (y % 2) * half, half, 0)
    qw = [lax.ppermute(qw_in, chip_x, t) for t in (TAKE_0, TAKE_1)]

    ids = jnp.pad(domain_ids.astype(BF).reshape(2, 256), ((0, 14), (0, 0)))
    lane = jnp.arange(HD, dtype=jnp.int32)
    bias = 0.5 * head_bias
    high = lax.reduce_precision(bias, 8, 7)
    coef = jnp.where(lane < 4, high[:, None], jnp.where(lane < 8, (bias - high)[:, None], 0.0))

    dy = jnp.array([0, 0, 1, 1, 3, 3, 2, 2], jnp.int32)
    dx = jnp.array([0, 1] * 4, jnp.int32)
    src_y = (y - dy) % NY
    at = jnp.sum(jnp.where(src_y[:, None] == jnp.arange(NY), block_order[None, :], 0), axis=1)
    key_at = at * 4 + (xh ^ dx) * 2 + core
    own_at = key_at[0]
    scal = jnp.concatenate([jnp.stack([z, core, xl, xl ^ xh, own_at, own_at ^ 1]), key_at, (y % 2)[None]])
    place = own_at * rows + jnp.arange(rows, dtype=jnp.int32)
    inv = lax.rsqrt((place + 1).astype(F32))[:, None]

    kvw_other = lax.ppermute(kvw, "core", SWAP)
    kv_w = [kvw, kvw_other]
    sums = project_most(scal, xs, kv_w, True)
    kv_keep, kv_send, squares = project_last(scal, 2, last, kv_w, sums)
    kv_got = lax.ppermute(kv_send, "xl", SWAP)
    sq = squares[0] + kv_got[rows : rows + 12].astype(F32).reshape(3, rows).sum(axis=0)
    row_scale = lax.rsqrt(sq * (1.0 / D) + norm_eps)[:, None]
    mine = ((kv_keep + kv_got[:rows].astype(F32)) * row_scale).astype(BF)
    other = lax.ppermute(mine, "z", [(i, i ^ 1) for i in range(NZ)])
    even = z % 2 == 0
    kv = jnp.concatenate([jnp.where(even, mine, other), jnp.where(even, other, mine)], axis=1)
    kv = jnp.concatenate([kv, ids], axis=0)
    kv_x = lax.ppermute(kv, "xh", SWAP)
    kv_up = shift(kv, "y", NY, 1)
    kv_down = shift(kv, "y", NY, -1)
    kv_far = shift(kv_up, "y", NY, 1)
    kv_x_up = shift(kv_x, "y", NY, 1)
    kv_x_down = shift(kv_x, "y", NY, -1)
    kv_x_far = shift(kv_x_down, "y", NY, -1)

    qw = jnp.concatenate(qw, axis=1)
    q_w = [qw, lax.ppermute(qw, "y", [(i, i ^ 1) for i in range(NY)])]
    q_w += [lax.ppermute(w, "core", SWAP) for w in q_w]
    q_keep, q_send = project_all(scal, 3, xs, last, q_w)
    q_got = lax.ppermute(q_send, "xl", SWAP)
    q = ((q_keep + q_got.astype(F32)) * (row_scale * (0.5 / math.sqrt(HD)))).astype(BF)
    q = jnp.concatenate([q, lax.optimization_barrier(ids)], axis=0)
    q_other = lax.ppermute(q, "core", SWAP)

    ow = [lax.ppermute(out_weight, chip_x, t) for t in (TAKE_0, TAKE_1)]

    part = attend(scal, coef, q, q_other, [kv, kv_up, kv_down], (0, 2, 4))[0]
    part = attend(scal, coef, q, q_other, [kv_x, kv_far, kv_x_up, kv_x_down], (1, 6, 3, 5), part)[0]
    mine, theirs = attend(scal, coef, q, q_other, [kv_x_far], (7,), part, True)
    back = lax.ppermute(theirs, "core", SWAP)
    attended = ((mine + back.astype(F32)) * inv).astype(BF)

    hs, h_last = ring(attended)
    ow_other = [lax.ppermute(w, "core", SWAP) for w in ow]
    o_w = [ow[0], ow_other[0], ow[1], ow_other[1]]
    sums = project_most(scal, hs, o_w, False)
    o_keep, o_send = project_last(scal, 3, h_last, o_w, sums)
    o_got = lax.ppermute(o_send, "xl", SWAP)
    return (o_keep + o_got.astype(F32)).astype(BF)


def solution(mesh):
    split = Mesh(mesh.devices.reshape(4, 2, 2, 2, 8), ("y", "xh", "core", "xl", "z"))
    r, c = ("y", "xh", "core"), ("xl", "z")
    w = ("xh", "core")
    return jax.shard_map(
        shards,
        mesh=split,
        in_specs=(P(r, c), P(r), P(), P(w, c), P(w, None, None, None), P(c), P(w, c)),
        out_specs=P(r, c),
        check_vma=False,
    )
```

profile of v0, /device:TPU:8, one launch (start us, length us, event | category | flops | bytes accessed | tf_op | source)
XLA Modules:
  0.0 143.2 jit_solution(8498769587045273321)
XLA Ops:
  0.0 2.0 %collective-permute-start = (bf16[512,256]{1,0:T(8,128)(2,1)}, bf16[512,256]{1,0:T(8,128)(2,1)S(1)}, u32[]{:S(2)}, u32[]{:S(2)}) collective-permute-start(bf16[512,256]{1,0:T(8,128)(2,1)} %refs_0_.3), channel_id=1, source_target_pairs={{0,1},{1,2},{2,3},{3,4},{4,5},{5,6},{6,7},{7,0},{8,9},{9,10},{10,1... | collective-permute-start | bytes 786440 | tf_op jit(solution)/shard_map/ppermute | solution.py:27
  2.0 4.0 %collective-permute-start.3 = (bf16[512,256]{1,0:T(8,128)(2,1)}, bf16[512,256]{1,0:T(8,128)(2,1)S(1)}, u32[]{:S(2)}, u32[]{:S(2)}) collective-permute-start(bf16[512,256]{1,0:T(8,128)(2,1)} %refs_0_.3), channel_id=1, source_target_pairs={{0,7},{1,0},{2,1},{3,2},{4,3},{5,4},{6,5},{7,6},{8,15},{9,8},{10,9... | collective-permute-start | bytes 786440 | tf_op jit(solution)/shard_map/ppermute | solution.py:27
  6.1 2.3 %constant_dynamic-slice_fusion.1 = (bf16[1024,1,1,128]{3,2,1,0:T(2,128)(2,1)S(1)}, bf16[1024,1,1,128]{3,2,1,0:T(2,128)(2,1)S(1)}) fusion(bf16[1024,8,2,128]{3,2,1,0:T(2,128)(2,1)} %param.13, s32[]{:T(128)S(6)} %select_n.86, s32[]{:T(128)S(6)} %select_n.88, s32[]{:T(128)S(6)} %select_n.89), kind=kLoop, calls=%fused_computation.26 | loop fusion | bytes 1048588 | tf_op jit(solution)/shard_map/dynamic_slice | solution.py:348
  8.5 0.7 collective-permute-start.13
  9.2 3.3 %collective-permute-done.refs_1_ = bf16[512,256]{1,0:T(8,128)(2,1)S(1)} collective-permute-done((bf16[512,256]{1,0:T(8,128)(2,1)}, bf16[512,256]{1,0:T(8,128)(2,1)S(1)}, u32[]{:S(2)}, u32[]{:S(2)}) %collective-permute-start) | collective-permute-done | bytes 262176 | tf_op jit(solution)/shard_map/ppermute | solution.py:27
  12.5 3.2 %collective-permute-start.4 = (bf16[512,256]{1,0:T(8,128)(2,1)S(1)}, bf16[512,256]{1,0:T(8,128)(2,1)}, u32[]{:S(2)}, u32[]{:S(2)}) collective-permute-start(bf16[512,256]{1,0:T(8,128)(2,1)S(1)} %collective-permute-done.3.refs_6_), channel_id=1, source_target_pairs={{0,7},{1,0},{2,1},{3,2},{4,3},{5,4},{6,5},{7,6},{8,15},{9,8},{10,9... | collective-permute-start | bytes 786440 | tf_op jit(solution)/shard_map/ppermute | solution.py:27
  15.7 0.7 constant_dynamic-slice_fusion.2
  16.4 3.6 %collective-permute-start.7 = (bf16[512,256]{1,0:T(8,128)(2,1)}, bf16[512,256]{1,0:T(8,128)(2,1)}, u32[]{:S(2)}, u32[]{:S(2)}) collective-permute-start(bf16[512,256]{1,0:T(8,128)(2,1)} %constant_dynamic-slice_fusion.2), channel_id=1, source_target_pairs={{0,0},{32,8},{8,32},{40,40},{1,1},{33,9},{9,33},{41,41},{2,2},{34,... | collective-permute-start | bytes 786440 | tf_op jit(solution)/shard_map/ppermute | solution.py:356
  20.0 2.0 %collective-permute-start.8 = (bf16[512,256]{1,0:T(8,128)(2,1)}, bf16[512,256]{1,0:T(8,128)(2,1)}, u32[]{:S(2)}, u32[]{:S(2)}) collective-permute-start(bf16[512,256]{1,0:T(8,128)(2,1)} %constant_dynamic-slice_fusion.2), channel_id=1, source_target_pairs={{8,0},{40,8},{0,32},{32,40},{9,1},{41,9},{1,33},{33,41},{10,2},{42... | collective-permute-start | bytes 786440 | tf_op jit(solution)/shard_map/ppermute | solution.py:356
  22.1 3.2 %collective-permute-start.5 = (bf16[512,256]{1,0:T(8,128)(2,1)}, bf16[512,256]{1,0:T(8,128)(2,1)S(1)}, u32[]{:S(2)}, u32[]{:S(2)}) collective-permute-start(bf16[512,256]{1,0:T(8,128)(2,1)} %collective-permute-done.4.refs_5_), channel_id=1, source_target_pairs={{0,7},{1,0},{2,1},{3,2},{4,3},{5,4},{6,5},{7,6},{8,15},{9,8},{10,9... | collective-permute-start | bytes 786440 | tf_op jit(solution)/shard_map/ppermute | solution.py:27
  25.4 1.0 constant_dynamic-update-slice_fusion.1
  26.5 0.8 collective-permute-done.8
  27.3 1.0 constant_dynamic-update-slice_fusion.refs_8_
  28.2 0.5 collective-permute-start.9
  28.8 1.1 collective-permute-done.2.refs_3_
  29.9 0.7 broadcast_select_fusion.1
  30.7 0.1 concatenate.18.scal
  30.8 2.8 %project_most.2 = (f32[512,256]{1,0:T(8,128)S(1)}, f32[8,512]{1,0:T(8,128)S(1)}) custom-call(s32[15]{0:T(128)S(1)} %concatenate.18.scal, bf16[512,256]{1,0:T(8,128)(2,1)S(1)} %copy-done.1, bf16[512,256]{1,0:T(8,128)(2,1)S(1)} %collective-permute-done.refs_1_, bf16[512,256]{1,0:T(8,128)(2,1)} %collective-permute-done.1.refs_2_, ...), custom_call_target="tpu_custom_call" | custom-call | flops 469762048 | bytes 1048576 | tf_op jit(solution)/shard_map/project_most/pallas_call | solution.py:153
  33.7 4.9 %collective-permute-done.6.refs_7_.refs_0_ = bf16[512,256]{1,0:T(8,128)(2,1)} collective-permute-done((bf16[512,256]{1,0:T(8,128)(2,1)}, bf16[512,256]{1,0:T(8,128)(2,1)}, u32[]{:S(2)}, u32[]{:S(2)}) %collective-permute-start.6) | collective-permute-done | bytes 262176 | tf_op jit(solution)/shard_map/ppermute | solution.py:38
  38.5 1.5 %project_last.2 = (f32[512,128]{1,0:T(8,128)S(1)}, bf16[528,128]{1,0:T(8,128)(2,1)S(1)}, f32[8,512]{1,0:T(8,128)S(1)}) custom-call(s32[15]{0:T(128)S(1)} %concatenate.18.scal, bf16[512,256]{1,0:T(8,128)(2,1)} %collective-permute-done.6.refs_7_.refs_0_, bf16[1024,256]{1,0:T(8,128)(2,1)S(1)} %collective-permute-done.13.refs_7_.refs_1_, ...), custom_call_target="tpu_custom_call" | custom-call | tf_op jit(solution)/shard_map/project_last/pallas_call | solution.py:180
  40.1 0.7 copy-done.2
  40.8 9.3 %collective-permute-start.15 = (bf16[528,128]{1,0:T(8,128)(2,1)S(1)}, bf16[528,128]{1,0:T(8,128)(2,1)S(1)}, u32[]{:S(2)}, u32[]{:S(2)}) collective-permute-start(bf16[528,128]{1,0:T(8,128)(2,1)S(1)} %get-tuple-element.21), channel_id=1, source_target_pairs={{0,8},{8,0},{1,9},{9,1},{2,10},{10,2},{3,11},{11,3},{4,12},{12,4},... | collective-permute-start | bytes 405512 | tf_op jit(solution)/shard_map/ppermute | solution.py:378
  50.1 0.5 collective-permute-start.11
  50.6 2.5 %collective-permute-done.15 = bf16[528,128]{1,0:T(8,128)(2,1)S(1)} collective-permute-done((bf16[528,128]{1,0:T(8,128)(2,1)S(1)}, bf16[528,128]{1,0:T(8,128)(2,1)S(1)}, u32[]{:S(2)}, u32[]{:S(2)}) %collective-permute-start.15) | collective-permute-done | bytes 135200 | tf_op jit(solution)/shard_map/ppermute | solution.py:378
  53.1 0.6 copy-done.3
  53.8 1.1 multiply_convert_fusion.2
  54.9 0.1 collective-permute-start.17
  55.0 1.2 multiply_subtract_fusion
  56.2 0.6 convert_element_type.39
  56.8 0.7 reshape.52
  57.5 2.9 %project_all.1 = (f32[512,256]{1,0:T(8,128)S(1)}, bf16[512,256]{1,0:T(8,128)(2,1)S(1)}) custom-call(s32[15]{0:T(128)S(1)} %concatenate.18.scal, bf16[512,256]{1,0:T(8,128)(2,1)S(1)} %copy-done.1, bf16[512,256]{1,0:T(8,128)(2,1)S(1)} %collective-permute-done.refs_1_, bf16[512,256]{1,0:T(8,128)(2,1)} %collective-permute-done.1.refs_2_, ...), custom_call_target="tpu_custom_call" | custom-call | flops 1073741824 | bytes 2097152 | tf_op jit(solution)/shard_map/project_all/pallas_call | solution.py:198
  60.4 2.1 %collective-permute-start.12 = (bf16[512,256]{1,0:T(8,128)(2,1)S(1)}, bf16[512,256]{1,0:T(8,128)(2,1)S(1)}, u32[]{:S(2)}, u32[]{:S(2)}) collective-permute-start(bf16[512,256]{1,0:T(8,128)(2,1)S(1)} %get-tuple-element.17), channel_id=1, source_target_pairs={{0,8},{8,0},{1,9},{9,1},{2,10},{10,2},{3,11},{11,3},{4,12},{12,4},... | collective-permute-start | bytes 786440 | tf_op jit(solution)/shard_map/ppermute | solution.py:398
  62.5 0.9 broadcast_select_fusion.3
  63.5 1.6 %collective-permute-start.18 = (bf16[528,256]{1,0:T(8,128)(2,1)S(1)}, bf16[528,256]{1,0:T(8,128)(2,1)S(1)}, u32[]{:S(2)}, u32[]{:S(2)}) collective-permute-start(bf16[528,256]{1,0:T(8,128)(2,1)S(1)} %pad_maximum_fusion.2.refs_0_), channel_id=1, source_target_pairs={{0,32},{32,0},{1,33},{33,1},{2,34},{34,2},{3,35},{35,3},{4,36},{36... | collective-permute-start | bytes 811016 | tf_op jit(solution)/shard_map/ppermute | solution.py:386
  65.1 2.4 %collective-permute-start.21 = (bf16[528,256]{1,0:T(8,128)(2,1)S(1)}, bf16[528,256]{1,0:T(8,128)(2,1)S(1)}, u32[]{:S(2)}, u32[]{:S(2)}) collective-permute-start(bf16[528,256]{1,0:T(8,128)(2,1)S(1)} %pad_maximum_fusion.2.refs_0_), channel_id=1, source_target_pairs={{0,64},{64,128},{128,192},{192,0},{1,65},{65,129},{129,193},{193,1... | collective-permute-start | bytes 811016 | tf_op jit(solution)/shard_map/ppermute | solution.py:27
  67.5 2.1 %collective-permute-done.12 = bf16[512,256]{1,0:T(8,128)(2,1)S(1)} collective-permute-done((bf16[512,256]{1,0:T(8,128)(2,1)S(1)}, bf16[512,256]{1,0:T(8,128)(2,1)S(1)}, u32[]{:S(2)}, u32[]{:S(2)}) %collective-permute-start.12) | collective-permute-done | bytes 262176 | tf_op jit(solution)/shard_map/ppermute | solution.py:398
  69.7 0.1 multiply_convert_fusion.1
  69.8 0.1 collective-permute-start.16
  70.0 4.9 %collective-permute-done.18.refs_0_ = bf16[528,256]{1,0:T(8,128)(2,1)S(1)} collective-permute-done((bf16[528,256]{1,0:T(8,128)(2,1)S(1)}, bf16[528,256]{1,0:T(8,128)(2,1)S(1)}, u32[]{:S(2)}, u32[]{:S(2)}) %collective-permute-start.18) | collective-permute-done | bytes 270368 | tf_op jit(solution)/shard_map/ppermute | solution.py:386
  74.9 0.4 collective-permute-start.19
  75.3 1.6 %collective-permute-start.23 = (bf16[528,256]{1,0:T(8,128)(2,1)S(1)}, bf16[528,256]{1,0:T(8,128)(2,1)S(1)}, u32[]{:S(2)}, u32[]{:S(2)}) collective-permute-start(bf16[528,256]{1,0:T(8,128)(2,1)S(1)} %collective-permute-done.18.refs_0_), channel_id=1, source_target_pairs={{0,64},{64,128},{128,192},{192,0},{1,65},{65,129},{129,193},{193,1... | collective-permute-start | bytes 811016 | tf_op jit(solution)/shard_map/ppermute | solution.py:27
  76.9 1.6 %collective-permute-start.22 = (bf16[528,256]{1,0:T(8,128)(2,1)S(1)}, bf16[528,256]{1,0:T(8,128)(2,1)S(1)}, u32[]{:S(2)}, u32[]{:S(2)}) collective-permute-start(bf16[528,256]{1,0:T(8,128)(2,1)S(1)} %collective-permute-done.21.refs_1_), channel_id=1, source_target_pairs={{0,64},{64,128},{128,192},{192,0},{1,65},{65,129},{129,193},{193,1... | collective-permute-start | bytes 811016 | tf_op jit(solution)/shard_map/ppermute | solution.py:27
  78.5 6.2 %attend.3.refs_4_ = f32[2,512,256]{2,1,0:T(8,128)S(1)} custom-call(s32[15]{0:T(128)S(1)} %concatenate.18.scal, f32[2,128]{1,0:T(2,128)S(1)} %select_select_fusion.coef_ref, bf16[528,256]{1,0:T(8,128)(2,1)S(1)} %pad_maximum_fusion.1.q_ref, bf16[528,256]{1,0:T(8,128)(2,1)S(1)} %collective-permute-done.16.q_other_ref, ...), custom_call_target="tpu_custom_call" | custom-call | flops 3221225472 | bytes 1048576 | tf_op jit(solution)/shard_map/attend/pallas_call | solution.py:326
  84.8 3.4 %collective-permute-done.22.refs_1_ = bf16[528,256]{1,0:T(8,128)(2,1)S(1)} collective-permute-done((bf16[528,256]{1,0:T(8,128)(2,1)S(1)}, bf16[528,256]{1,0:T(8,128)(2,1)S(1)}, u32[]{:S(2)}, u32[]{:S(2)}) %collective-permute-start.22) | collective-permute-done | bytes 270368 | tf_op jit(solution)/shard_map/ppermute | solution.py:27
  88.2 5.0 %attend.4.refs_1_ = f32[2,512,256]{2,1,0:T(8,128)S(1)} custom-call(s32[15]{0:T(128)S(1)} %concatenate.18.scal, f32[2,128]{1,0:T(2,128)S(1)} %select_select_fusion.coef_ref, bf16[528,256]{1,0:T(8,128)(2,1)S(1)} %pad_maximum_fusion.1.q_ref, bf16[528,256]{1,0:T(8,128)(2,1)S(1)} %collective-permute-done.16.q_other_ref, ...), custom_call_target="tpu_custom_call" | custom-call | flops 4294967296 | bytes 1048576 | tf_op jit(solution)/shard_map/attend/pallas_call | solution.py:326
  93.3 2.5 %attend.5 = (f32[512,256]{1,0:T(8,128)S(1)}, bf16[512,256]{1,0:T(8,128)(2,1)S(1)}) custom-call(s32[15]{0:T(128)S(1)} %concatenate.18.scal, f32[2,128]{1,0:T(2,128)S(1)} %select_select_fusion.coef_ref, bf16[528,256]{1,0:T(8,128)(2,1)S(1)} %pad_maximum_fusion.1.q_ref, bf16[528,256]{1,0:T(8,128)(2,1)S(1)} %collective-permute-done.16.q_other_ref, ...), custom_call_target="tpu_custom_call" | custom-call | flops 1073741824 | bytes 1048576 | tf_op jit(solution)/shard_map/attend/pallas_call | solution.py:326
  96.0 1.5 %collective-permute-done.25 = bf16[512,256]{1,0:T(8,128)(2,1)S(1)} collective-permute-done((bf16[512,256]{1,0:T(8,128)(2,1)S(1)}, bf16[512,256]{1,0:T(8,128)(2,1)S(1)}, u32[]{:S(2)}, u32[]{:S(2)}) %collective-permute-start.25) | collective-permute-done | bytes 262176 | tf_op jit(solution)/shard_map/ppermute | solution.py:408
  97.4 0.1 multiply_convert_fusion.refs_0_
  97.6 1.5 %collective-permute-start.26 = (bf16[512,256]{1,0:T(8,128)(2,1)S(1)}, bf16[512,256]{1,0:T(8,128)(2,1)S(1)}, u32[]{:S(2)}, u32[]{:S(2)}) collective-permute-start(bf16[512,256]{1,0:T(8,128)(2,1)S(1)} %multiply_convert_fusion.refs_0_), channel_id=1, source_target_pairs={{0,1},{1,2},{2,3},{3,4},{4,5},{5,6},{6,7},{7,0},{8,9},{9,10},{10,1... | collective-permute-start | bytes 786440 | tf_op jit(solution)/shard_map/ppermute | solution.py:27
  99.1 2.2 %collective-permute-start.29 = (bf16[512,256]{1,0:T(8,128)(2,1)S(1)}, bf16[512,256]{1,0:T(8,128)(2,1)S(1)}, u32[]{:S(2)}, u32[]{:S(2)}) collective-permute-start(bf16[512,256]{1,0:T(8,128)(2,1)S(1)} %multiply_convert_fusion.refs_0_), channel_id=1, source_target_pairs={{0,7},{1,0},{2,1},{3,2},{4,3},{5,4},{6,5},{7,6},{8,15},{9,8},{10,9... | collective-permute-start | bytes 786440 | tf_op jit(solution)/shard_map/ppermute | solution.py:27
  101.4 0.7 collective-permute-start.33
  102.0 3.9 %collective-permute-start.35 = (bf16[1024,256]{1,0:T(8,128)(2,1)S(1)}, bf16[1024,256]{1,0:T(8,128)(2,1)S(1)}, u32[]{:S(2)}, u32[]{:S(2)}) collective-permute-start(bf16[1024,256]{1,0:T(8,128)(2,1)S(1)} %copy-done.8), channel_id=1, source_target_pairs={{8,0},{40,8},{0,32},{32,40},{9,1},{41,9},{1,33},{33,41},{10,2},{42... | collective-permute-start | bytes 1572872 | tf_op jit(solution)/shard_map/ppermute | solution.py:403
  106.0 1.9 %collective-permute-done.26.refs_1_ = bf16[512,256]{1,0:T(8,128)(2,1)S(1)} collective-permute-done((bf16[512,256]{1,0:T(8,128)(2,1)S(1)}, bf16[512,256]{1,0:T(8,128)(2,1)S(1)}, u32[]{:S(2)}, u32[]{:S(2)}) %collective-permute-start.26) | collective-permute-done | bytes 262176 | tf_op jit(solution)/shard_map/ppermute | solution.py:27
  107.9 3.2 %collective-permute-start.30 = (bf16[512,256]{1,0:T(8,128)(2,1)S(1)}, bf16[512,256]{1,0:T(8,128)(2,1)S(1)}, u32[]{:S(2)}, u32[]{:S(2)}) collective-permute-start(bf16[512,256]{1,0:T(8,128)(2,1)S(1)} %collective-permute-done.29.refs_6_), channel_id=1, source_target_pairs={{0,7},{1,0},{2,1},{3,2},{4,3},{5,4},{6,5},{7,6},{8,15},{9,8},{10,9... | collective-permute-start | bytes 786440 | tf_op jit(solution)/shard_map/ppermute | solution.py:27
  111.1 5.7 %collective-permute-done.27.refs_2_ = bf16[512,256]{1,0:T(8,128)(2,1)S(1)} collective-permute-done((bf16[512,256]{1,0:T(8,128)(2,1)S(1)}, bf16[512,256]{1,0:T(8,128)(2,1)S(1)}, u32[]{:S(2)}, u32[]{:S(2)}) %collective-permute-start.27) | collective-permute-done | bytes 262176 | tf_op jit(solution)/shard_map/ppermute | solution.py:27
  116.9 3.2 %collective-permute-start.31 = (bf16[512,256]{1,0:T(8,128)(2,1)S(1)}, bf16[512,256]{1,0:T(8,128)(2,1)S(1)}, u32[]{:S(2)}, u32[]{:S(2)}) collective-permute-start(bf16[512,256]{1,0:T(8,128)(2,1)S(1)} %collective-permute-done.30.refs_5_), channel_id=1, source_target_pairs={{0,7},{1,0},{2,1},{3,2},{4,3},{5,4},{6,5},{7,6},{8,15},{9,8},{10,9... | collective-permute-start | bytes 786440 | tf_op jit(solution)/shard_map/ppermute | solution.py:27
  120.1 0.5 collective-permute-start.36
  120.6 4.4 %collective-permute-done.28.refs_3_ = bf16[512,256]{1,0:T(8,128)(2,1)S(1)} collective-permute-done((bf16[512,256]{1,0:T(8,128)(2,1)S(1)}, bf16[512,256]{1,0:T(8,128)(2,1)S(1)}, u32[]{:S(2)}, u32[]{:S(2)}) %collective-permute-start.28) | collective-permute-done | bytes 262176 | tf_op jit(solution)/shard_map/ppermute | solution.py:27
  125.1 2.0 %project_most.3.refs_5_ = f32[512,512]{1,0:T(8,128)S(1)} custom-call(s32[15]{0:T(128)S(1)} %concatenate.18.scal, bf16[512,256]{1,0:T(8,128)(2,1)S(1)} %multiply_convert_fusion.refs_0_, bf16[512,256]{1,0:T(8,128)(2,1)S(1)} %collective-permute-done.26.refs_1_, bf16[512,256]{1,0:T(8,128)(2,1)S(1)} %collective-permute-done.27.refs_2_, ...), custom_call_target="tpu_custom_call" | custom-call | flops 939524096 | bytes 2097152 | tf_op jit(solution)/shard_map/project_most/pallas_call | solution.py:153
  127.2 5.5 %collective-permute-done.32.refs_0_ = bf16[512,256]{1,0:T(8,128)(2,1)S(1)} collective-permute-done((bf16[512,256]{1,0:T(8,128)(2,1)S(1)}, bf16[512,256]{1,0:T(8,128)(2,1)S(1)}, u32[]{:S(2)}, u32[]{:S(2)}) %collective-permute-start.32) | collective-permute-done | bytes 262176 | tf_op jit(solution)/shard_map/ppermute | solution.py:38
  132.7 0.9 project_last.3
  133.6 4.4 %collective-permute-start.37 = (bf16[512,256]{1,0:T(8,128)(2,1)S(1)}, bf16[512,256]{1,0:T(8,128)(2,1)S(1)}, u32[]{:S(2)}, u32[]{:S(2)}) collective-permute-start(bf16[512,256]{1,0:T(8,128)(2,1)S(1)} %get-tuple-element.26), channel_id=1, source_target_pairs={{0,8},{8,0},{1,9},{9,1},{2,10},{10,2},{3,11},{11,3},{4,12},{12,4},... | collective-permute-start | bytes 786440 | tf_op jit(solution)/shard_map/ppermute | solution.py:416
  138.0 4.4 %collective-permute-done.37 = bf16[512,256]{1,0:T(8,128)(2,1)S(1)} collective-permute-done((bf16[512,256]{1,0:T(8,128)(2,1)S(1)}, bf16[512,256]{1,0:T(8,128)(2,1)S(1)}, u32[]{:S(2)}, u32[]{:S(2)}) %collective-permute-start.37) | collective-permute-done | bytes 262176 | tf_op jit(solution)/shard_map/ppermute | solution.py:416
  142.5 0.8 add_convert_fusion
  (73 shorter events, 1.0 us)
Async XLA Ops:
  0.0 15.7 %copy-start = (bf16[1024,256]{1,0:T(8,128)(2,1)S(1)}, bf16[1024,256]{1,0:T(8,128)(2,1)}, u32[]{:S(2)}) copy-start(bf16[1024,256]{1,0:T(8,128)(2,1)} %param.12) | copy-start | bytes 1572868
  0.0 22.0 %copy-start.10 = (s32[8]{0:T(128)S(1)}, s32[8]{0:T(128)}, u32[]{:S(2)}) copy-start(s32[8]{0:T(128)} %constant.112) | copy-start | bytes 100
  0.0 30.6 %copy-start.5 = (s32[8]{0:T(128)S(1)}, s32[8]{0:T(128)}, u32[]{:S(2)}) copy-start(s32[8]{0:T(128)} %constant.108.clone) | copy-start | bytes 100
  0.0 30.8 %copy-start.1 = (bf16[512,256]{1,0:T(8,128)(2,1)S(1)}, bf16[512,256]{1,0:T(8,128)(2,1)}, u32[]{:S(2)}) copy-start(bf16[512,256]{1,0:T(8,128)(2,1)} %refs_0_.3) | copy-start | bytes 786436
  0.0 25.3 %copy-start.9 = (s32[4]{0:T(128)S(1)}, s32[4]{0:T(128)}, u32[]{:S(2)}) copy-start(s32[4]{0:T(128)} %param.11) | copy-start | bytes 52
  0.0 12.4 %collective-permute-start = (bf16[512,256]{1,0:T(8,128)(2,1)}, bf16[512,256]{1,0:T(8,128)(2,1)S(1)}, u32[]{:S(2)}, u32[]{:S(2)}) collective-permute-start(bf16[512,256]{1,0:T(8,128)(2,1)} %refs_0_.3), channel_id=1, source_target_pairs={{0,1},{1,2},{2,3},{3,4},{4,5},{5,6},{6,7},{7,0},{8,9},{9,10},{10,1... | collective-permute-start | bytes 786440 | tf_op jit(solution)/shard_map/ppermute | solution.py:27
  2.0 10.5 %collective-permute-start.3 = (bf16[512,256]{1,0:T(8,128)(2,1)}, bf16[512,256]{1,0:T(8,128)(2,1)S(1)}, u32[]{:S(2)}, u32[]{:S(2)}) collective-permute-start(bf16[512,256]{1,0:T(8,128)(2,1)} %refs_0_.3), channel_id=1, source_target_pairs={{0,7},{1,0},{2,1},{3,2},{4,3},{5,4},{6,5},{7,6},{8,15},{9,8},{10,9... | collective-permute-start | bytes 786440 | tf_op jit(solution)/shard_map/ppermute | solution.py:27
  8.4 47.8 %copy-start.4 = (s32[512]{0:T(512)S(1)}, s32[512]{0:T(512)}, u32[]{:S(2)}) copy-start(s32[512]{0:T(512)} %param.10) | copy-start | bytes 6148
  8.5 17.9 %collective-permute-start.13 = (bf16[1024,256]{1,0:T(8,128)(2,1)S(1)}, bf16[1024,256]{1,0:T(8,128)(2,1)S(1)}, u32[]{:S(2)}, u32[]{:S(2)}) collective-permute-start(bf16[1024,256]{1,0:T(8,128)(2,1)S(1)} %pad_maximum_fusion), channel_id=1, source_target_pairs={{0,0},{32,8},{8,32},{40,40},{1,1},{33,9},{9,33},{41,41},{2,2},{34,... | collective-permute-start | bytes 1572872 | tf_op jit(solution)/shard_map/ppermute | solution.py:353
  12.5 9.5 %collective-permute-start.1 = (bf16[512,256]{1,0:T(8,128)(2,1)S(1)}, bf16[512,256]{1,0:T(8,128)(2,1)}, u32[]{:S(2)}, u32[]{:S(2)}) collective-permute-start(bf16[512,256]{1,0:T(8,128)(2,1)S(1)} %collective-permute-done.refs_1_), channel_id=1, source_target_pairs={{0,1},{1,2},{2,3},{3,4},{4,5},{5,6},{6,7},{7,0},{8,9},{9,10},{10,1... | collective-permute-start | bytes 786440 | tf_op jit(solution)/shard_map/ppermute | solution.py:27
  12.5 9.6 %collective-permute-start.4 = (bf16[512,256]{1,0:T(8,128)(2,1)S(1)}, bf16[512,256]{1,0:T(8,128)(2,1)}, u32[]{:S(2)}, u32[]{:S(2)}) collective-permute-start(bf16[512,256]{1,0:T(8,128)(2,1)S(1)} %collective-permute-done.3.refs_6_), channel_id=1, source_target_pairs={{0,7},{1,0},{2,1},{3,2},{4,3},{5,4},{6,5},{7,6},{8,15},{9,8},{10,9... | collective-permute-start | bytes 786440 | tf_op jit(solution)/shard_map/ppermute | solution.py:27
  16.4 9.0 %collective-permute-start.7 = (bf16[512,256]{1,0:T(8,128)(2,1)}, bf16[512,256]{1,0:T(8,128)(2,1)}, u32[]{:S(2)}, u32[]{:S(2)}) collective-permute-start(bf16[512,256]{1,0:T(8,128)(2,1)} %constant_dynamic-slice_fusion.2), channel_id=1, source_target_pairs={{0,0},{32,8},{8,32},{40,40},{1,1},{33,9},{9,33},{41,41},{2,2},{34,... | collective-permute-start | bytes 786440 | tf_op jit(solution)/shard_map/ppermute | solution.py:356
  20.0 7.2 %collective-permute-start.8 = (bf16[512,256]{1,0:T(8,128)(2,1)}, bf16[512,256]{1,0:T(8,128)(2,1)}, u32[]{:S(2)}, u32[]{:S(2)}) collective-permute-start(bf16[512,256]{1,0:T(8,128)(2,1)} %constant_dynamic-slice_fusion.2), channel_id=1, source_target_pairs={{8,0},{40,8},{0,32},{32,40},{9,1},{41,9},{1,33},{33,41},{10,2},{42... | collective-permute-start | bytes 786440 | tf_op jit(solution)/shard_map/ppermute | solution.py:356
  22.0 7.9 %collective-permute-start.2 = (bf16[512,256]{1,0:T(8,128)(2,1)}, bf16[512,256]{1,0:T(8,128)(2,1)S(1)}, u32[]{:S(2)}, u32[]{:S(2)}) collective-permute-start(bf16[512,256]{1,0:T(8,128)(2,1)} %collective-permute-done.1.refs_2_), channel_id=1, source_target_pairs={{0,1},{1,2},{2,3},{3,4},{4,5},{5,6},{6,7},{7,0},{8,9},{9,10},{10,1... | collective-permute-start | bytes 786440 | tf_op jit(solution)/shard_map/ppermute | solution.py:27
  22.1 7.8 %collective-permute-start.5 = (bf16[512,256]{1,0:T(8,128)(2,1)}, bf16[512,256]{1,0:T(8,128)(2,1)S(1)}, u32[]{:S(2)}, u32[]{:S(2)}) collective-permute-start(bf16[512,256]{1,0:T(8,128)(2,1)} %collective-permute-done.4.refs_5_), channel_id=1, source_target_pairs={{0,7},{1,0},{2,1},{3,2},{4,3},{5,4},{6,5},{7,6},{8,15},{9,8},{10,9... | collective-permute-start | bytes 786440 | tf_op jit(solution)/shard_map/ppermute | solution.py:27
  26.4 4.4 %collective-permute-start.14 = (bf16[1024,256]{1,0:T(8,128)(2,1)S(1)}, bf16[1024,256]{1,0:T(8,128)(2,1)S(1)}, u32[]{:S(2)}, u32[]{:S(2)}) collective-permute-start(bf16[1024,256]{1,0:T(8,128)(2,1)S(1)} %collective-permute-done.13.refs_7_.refs_1_), channel_id=1, source_target_pairs={{0,16},{16,0},{1,17},{17,1},{2,18},{18,2},{3,19},{19,3},{4,20},{20... | collective-permute-start | bytes 1572872 | tf_op jit(solution)/shard_map/ppermute | solution.py:374
  28.2 21.9 %collective-permute-start.9 = (bf16[512,512]{1,0:T(8,128)(2,1)S(1)}, bf16[512,512]{1,0:T(8,128)(2,1)}, u32[]{:S(2)}, u32[]{:S(2)}) collective-permute-start(bf16[512,512]{1,0:T(8,128)(2,1)S(1)} %constant_dynamic-update-slice_fusion.refs_8_), channel_id=1, source_target_pairs={{0,64},{64,0},{128,192},{192,128},{1,65},{65,1},{129,193},{193,129... | collective-permute-start | bytes 1572872 | tf_op jit(solution)/shard_map/ppermute | solution.py:395
  30.6 7.9 %collective-permute-start.6 = (bf16[512,256]{1,0:T(8,128)(2,1)}, bf16[512,256]{1,0:T(8,128)(2,1)}, u32[]{:S(2)}, u32[]{:S(2)}) collective-permute-start(bf16[512,256]{1,0:T(8,128)(2,1)} %broadcast_select_fusion.1), channel_id=1, source_target_pairs={{0,1},{1,2},{2,3},{3,4},{4,5},{5,6},{6,7},{7,0},{16,23},{17,16},{1... | collective-permute-start | bytes 786440 | tf_op jit(solution)/shard_map/ppermute | solution.py:38
  40.1 0.7 copy-start.2
  40.8 12.3 %collective-permute-start.15 = (bf16[528,128]{1,0:T(8,128)(2,1)S(1)}, bf16[528,128]{1,0:T(8,128)(2,1)S(1)}, u32[]{:S(2)}, u32[]{:S(2)}) collective-permute-start(bf16[528,128]{1,0:T(8,128)(2,1)S(1)} %get-tuple-element.21), channel_id=1, source_target_pairs={{0,8},{8,0},{1,9},{9,1},{2,10},{10,2},{3,11},{11,3},{4,12},{12,4},... | collective-permute-start | bytes 405512 | tf_op jit(solution)/shard_map/ppermute | solution.py:378
  50.1 7.4 %collective-permute-start.10 = (bf16[512,512]{1,0:T(8,128)(2,1)S(1)}, bf16[512,512]{1,0:T(8,128)(2,1)S(1)}, u32[]{:S(2)}, u32[]{:S(2)}) collective-permute-start(bf16[512,512]{1,0:T(8,128)(2,1)S(1)} %constant_dynamic-update-slice_fusion.refs_8_), channel_id=1, source_target_pairs={{0,16},{16,0},{1,17},{17,1},{2,18},{18,2},{3,19},{19,3},{4,20},{20... | collective-permute-start | bytes 1572872 | tf_op jit(solution)/shard_map/ppermute | solution.py:396
  50.1 7.4 %collective-permute-start.11 = (bf16[512,512]{1,0:T(8,128)(2,1)}, bf16[512,512]{1,0:T(8,128)(2,1)S(1)}, u32[]{:S(2)}, u32[]{:S(2)}) collective-permute-start(bf16[512,512]{1,0:T(8,128)(2,1)} %collective-permute-done.9.refs_9_), channel_id=1, source_target_pairs={{0,16},{16,0},{1,17},{17,1},{2,18},{18,2},{3,19},{19,3},{4,20},{20... | collective-permute-start | bytes 1572872 | tf_op jit(solution)/shard_map/ppermute | solution.py:396
  53.1 0.6 copy-start.3
  54.9 7.6 %collective-permute-start.17 = (bf16[512,128]{1,0:T(8,128)(2,1)S(1)}, bf16[512,128]{1,0:T(8,128)(2,1)}, u32[]{:S(2)}, u32[]{:S(2)}) collective-permute-start(bf16[512,128]{1,0:T(8,128)(2,1)S(1)} %multiply_convert_fusion.2), channel_id=1, source_target_pairs={{0,1},{1,0},{2,3},{3,2},{4,5},{5,4},{6,7},{7,6},{8,9},{9,8},{10,11... | collective-permute-start | bytes 393224 | tf_op jit(solution)/shard_map/ppermute | solution.py:382
  57.5 12.5 %copy-start.6 = (f32[2]{0:T(128)S(1)}, f32[2]{0:T(128)}, u32[]{:S(2)}) copy-start(f32[2]{0:T(128)} %get-tuple-element.33) | copy-start | bytes 28
  57.5 12.5 %copy-start.7 = (f32[2]{0:T(128)S(1)}, f32[2]{0:T(128)}, u32[]{:S(2)}) copy-start(f32[2]{0:T(128)} %get-tuple-element.34) | copy-start | bytes 28
  60.4 9.3 %collective-permute-start.12 = (bf16[512,256]{1,0:T(8,128)(2,1)S(1)}, bf16[512,256]{1,0:T(8,128)(2,1)S(1)}, u32[]{:S(2)}, u32[]{:S(2)}) collective-permute-start(bf16[512,256]{1,0:T(8,128)(2,1)S(1)} %get-tuple-element.17), channel_id=1, source_target_pairs={{0,8},{8,0},{1,9},{9,1},{2,10},{10,2},{3,11},{11,3},{4,12},{12,4},... | collective-permute-start | bytes 786440 | tf_op jit(solution)/shard_map/ppermute | solution.py:398
  63.5 11.4 %collective-permute-start.18 = (bf16[528,256]{1,0:T(8,128)(2,1)S(1)}, bf16[528,256]{1,0:T(8,128)(2,1)S(1)}, u32[]{:S(2)}, u32[]{:S(2)}) collective-permute-start(bf16[528,256]{1,0:T(8,128)(2,1)S(1)} %pad_maximum_fusion.2.refs_0_), channel_id=1, source_target_pairs={{0,32},{32,0},{1,33},{33,1},{2,34},{34,2},{3,35},{35,3},{4,36},{36... | collective-permute-start | bytes 811016 | tf_op jit(solution)/shard_map/ppermute | solution.py:386
  65.1 11.8 %collective-permute-start.21 = (bf16[528,256]{1,0:T(8,128)(2,1)S(1)}, bf16[528,256]{1,0:T(8,128)(2,1)S(1)}, u32[]{:S(2)}, u32[]{:S(2)}) collective-permute-start(bf16[528,256]{1,0:T(8,128)(2,1)S(1)} %pad_maximum_fusion.2.refs_0_), channel_id=1, source_target_pairs={{0,64},{64,128},{128,192},{192,0},{1,65},{65,129},{129,193},{193,1... | collective-permute-start | bytes 811016 | tf_op jit(solution)/shard_map/ppermute | solution.py:27
  67.5 11.0 %collective-permute-start.24 = (bf16[528,256]{1,0:T(8,128)(2,1)S(1)}, bf16[528,256]{1,0:T(8,128)(2,1)S(1)}, u32[]{:S(2)}, u32[]{:S(2)}) collective-permute-start(bf16[528,256]{1,0:T(8,128)(2,1)S(1)} %pad_maximum_fusion.2.refs_0_), channel_id=1, source_target_pairs={{0,192},{64,0},{128,64},{192,128},{1,193},{65,1},{129,65},{193,129... | collective-permute-start | bytes 811016 | tf_op jit(solution)/shard_map/ppermute | solution.py:27
  69.8 8.7 %collective-permute-start.16 = (bf16[528,256]{1,0:T(8,128)(2,1)S(1)}, bf16[528,256]{1,0:T(8,128)(2,1)S(1)}, u32[]{:S(2)}, u32[]{:S(2)}) collective-permute-start(bf16[528,256]{1,0:T(8,128)(2,1)S(1)} %pad_maximum_fusion.1.q_ref), channel_id=1, source_target_pairs={{0,16},{16,0},{1,17},{17,1},{2,18},{18,2},{3,19},{19,3},{4,20},{20... | collective-permute-start | bytes 811016 | tf_op jit(solution)/shard_map/ppermute | solution.py:401
  74.9 9.9 %collective-permute-start.19 = (bf16[528,256]{1,0:T(8,128)(2,1)S(1)}, bf16[528,256]{1,0:T(8,128)(2,1)S(1)}, u32[]{:S(2)}, u32[]{:S(2)}) collective-permute-start(bf16[528,256]{1,0:T(8,128)(2,1)S(1)} %collective-permute-done.18.refs_0_), channel_id=1, source_target_pairs={{0,192},{64,0},{128,64},{192,128},{1,193},{65,1},{129,65},{193,129... | collective-permute-start | bytes 811016 | tf_op jit(solution)/shard_map/ppermute | solution.py:27
  75.3 12.9 %collective-permute-start.23 = (bf16[528,256]{1,0:T(8,128)(2,1)S(1)}, bf16[528,256]{1,0:T(8,128)(2,1)S(1)}, u32[]{:S(2)}, u32[]{:S(2)}) collective-permute-start(bf16[528,256]{1,0:T(8,128)(2,1)S(1)} %collective-permute-done.18.refs_0_), channel_id=1, source_target_pairs={{0,64},{64,128},{128,192},{192,0},{1,65},{65,129},{129,193},{193,1... | collective-permute-start | bytes 811016 | tf_op jit(solution)/shard_map/ppermute | solution.py:27
  76.9 11.3 %collective-permute-start.22 = (bf16[528,256]{1,0:T(8,128)(2,1)S(1)}, bf16[528,256]{1,0:T(8,128)(2,1)S(1)}, u32[]{:S(2)}, u32[]{:S(2)}) collective-permute-start(bf16[528,256]{1,0:T(8,128)(2,1)S(1)} %collective-permute-done.21.refs_1_), channel_id=1, source_target_pairs={{0,64},{64,128},{128,192},{192,0},{1,65},{65,129},{129,193},{193,1... | collective-permute-start | bytes 811016 | tf_op jit(solution)/shard_map/ppermute | solution.py:27
  84.8 8.5 %collective-permute-start.20 = (bf16[528,256]{1,0:T(8,128)(2,1)S(1)}, bf16[528,256]{1,0:T(8,128)(2,1)S(1)}, u32[]{:S(2)}, u32[]{:S(2)}) collective-permute-start(bf16[528,256]{1,0:T(8,128)(2,1)S(1)} %collective-permute-done.19.refs_3_), channel_id=1, source_target_pairs={{0,192},{64,0},{128,64},{192,128},{1,193},{65,1},{129,65},{193,129... | collective-permute-start | bytes 811016 | tf_op jit(solution)/shard_map/ppermute | solution.py:27
  93.3 8.1 %copy-start.8 = (bf16[1024,256]{1,0:T(8,128)(2,1)S(1)}, bf16[1024,256]{1,0:T(8,128)(2,1)}, u32[]{:S(2)}) copy-start(bf16[1024,256]{1,0:T(8,128)(2,1)} %param.15) | copy-start | bytes 1572868
  95.8 1.6 %collective-permute-start.25 = (bf16[512,256]{1,0:T(8,128)(2,1)S(1)}, bf16[512,256]{1,0:T(8,128)(2,1)S(1)}, u32[]{:S(2)}, u32[]{:S(2)}) collective-permute-start(bf16[512,256]{1,0:T(8,128)(2,1)S(1)} %get-tuple-element.24), channel_id=1, source_target_pairs={{0,16},{16,0},{1,17},{17,1},{2,18},{18,2},{3,19},{19,3},{4,20},{20... | collective-permute-start | bytes 786440 | tf_op jit(solution)/shard_map/ppermute | solution.py:408
  97.6 10.3 %collective-permute-start.26 = (bf16[512,256]{1,0:T(8,128)(2,1)S(1)}, bf16[512,256]{1,0:T(8,128)(2,1)S(1)}, u32[]{:S(2)}, u32[]{:S(2)}) collective-permute-start(bf16[512,256]{1,0:T(8,128)(2,1)S(1)} %multiply_convert_fusion.refs_0_), channel_id=1, source_target_pairs={{0,1},{1,2},{2,3},{3,4},{4,5},{5,6},{6,7},{7,0},{8,9},{9,10},{10,1... | collective-permute-start | bytes 786440 | tf_op jit(solution)/shard_map/ppermute | solution.py:27
  99.1 8.8 %collective-permute-start.29 = (bf16[512,256]{1,0:T(8,128)(2,1)S(1)}, bf16[512,256]{1,0:T(8,128)(2,1)S(1)}, u32[]{:S(2)}, u32[]{:S(2)}) collective-permute-start(bf16[512,256]{1,0:T(8,128)(2,1)S(1)} %multiply_convert_fusion.refs_0_), channel_id=1, source_target_pairs={{0,7},{1,0},{2,1},{3,2},{4,3},{5,4},{6,5},{7,6},{8,15},{9,8},{10,9... | collective-permute-start | bytes 786440 | tf_op jit(solution)/shard_map/ppermute | solution.py:27
  101.4 18.7 %collective-permute-start.33 = (bf16[1024,256]{1,0:T(8,128)(2,1)S(1)}, bf16[1024,256]{1,0:T(8,128)(2,1)S(1)}, u32[]{:S(2)}, u32[]{:S(2)}) collective-permute-start(bf16[1024,256]{1,0:T(8,128)(2,1)S(1)} %copy-done.8), channel_id=1, source_target_pairs={{0,0},{32,8},{8,32},{40,40},{1,1},{33,9},{9,33},{41,41},{2,2},{34,... | collective-permute-start | bytes 1572872 | tf_op jit(solution)/shard_map/ppermute | solution.py:403
  102.0 18.1 %collective-permute-start.35 = (bf16[1024,256]{1,0:T(8,128)(2,1)S(1)}, bf16[1024,256]{1,0:T(8,128)(2,1)S(1)}, u32[]{:S(2)}, u32[]{:S(2)}) collective-permute-start(bf16[1024,256]{1,0:T(8,128)(2,1)S(1)} %copy-done.8), channel_id=1, source_target_pairs={{8,0},{40,8},{0,32},{32,40},{9,1},{41,9},{1,33},{33,41},{10,2},{42... | collective-permute-start | bytes 1572872 | tf_op jit(solution)/shard_map/ppermute | solution.py:403
  107.9 9.0 %collective-permute-start.27 = (bf16[512,256]{1,0:T(8,128)(2,1)S(1)}, bf16[512,256]{1,0:T(8,128)(2,1)S(1)}, u32[]{:S(2)}, u32[]{:S(2)}) collective-permute-start(bf16[512,256]{1,0:T(8,128)(2,1)S(1)} %collective-permute-done.26.refs_1_), channel_id=1, source_target_pairs={{0,1},{1,2},{2,3},{3,4},{4,5},{5,6},{6,7},{7,0},{8,9},{9,10},{10,1... | collective-permute-start | bytes 786440 | tf_op jit(solution)/shard_map/ppermute | solution.py:27
  107.9 9.0 %collective-permute-start.30 = (bf16[512,256]{1,0:T(8,128)(2,1)S(1)}, bf16[512,256]{1,0:T(8,128)(2,1)S(1)}, u32[]{:S(2)}, u32[]{:S(2)}) collective-permute-start(bf16[512,256]{1,0:T(8,128)(2,1)S(1)} %collective-permute-done.29.refs_6_), channel_id=1, source_target_pairs={{0,7},{1,0},{2,1},{3,2},{4,3},{5,4},{6,5},{7,6},{8,15},{9,8},{10,9... | collective-permute-start | bytes 786440 | tf_op jit(solution)/shard_map/ppermute | solution.py:27
  116.9 8.1 %collective-permute-start.28 = (bf16[512,256]{1,0:T(8,128)(2,1)S(1)}, bf16[512,256]{1,0:T(8,128)(2,1)S(1)}, u32[]{:S(2)}, u32[]{:S(2)}) collective-permute-start(bf16[512,256]{1,0:T(8,128)(2,1)S(1)} %collective-permute-done.27.refs_2_), channel_id=1, source_target_pairs={{0,1},{1,2},{2,3},{3,4},{4,5},{5,6},{6,7},{7,0},{8,9},{9,10},{10,1... | collective-permute-start | bytes 786440 | tf_op jit(solution)/shard_map/ppermute | solution.py:27
  116.9 8.1 %collective-permute-start.31 = (bf16[512,256]{1,0:T(8,128)(2,1)S(1)}, bf16[512,256]{1,0:T(8,128)(2,1)S(1)}, u32[]{:S(2)}, u32[]{:S(2)}) collective-permute-start(bf16[512,256]{1,0:T(8,128)(2,1)S(1)} %collective-permute-done.30.refs_5_), channel_id=1, source_target_pairs={{0,7},{1,0},{2,1},{3,2},{4,3},{5,4},{6,5},{7,6},{8,15},{9,8},{10,9... | collective-permute-start | bytes 786440 | tf_op jit(solution)/shard_map/ppermute | solution.py:27
  120.1 5.0 %collective-permute-start.34 = (bf16[1024,256]{1,0:T(8,128)(2,1)S(1)}, bf16[1024,256]{1,0:T(8,128)(2,1)S(1)}, u32[]{:S(2)}, u32[]{:S(2)}) collective-permute-start(bf16[1024,256]{1,0:T(8,128)(2,1)S(1)} %collective-permute-done.33.refs_7_.refs_1_), channel_id=1, source_target_pairs={{0,16},{16,0},{1,17},{17,1},{2,18},{18,2},{3,19},{19,3},{4,20},{20... | collective-permute-start | bytes 1572872 | tf_op jit(solution)/shard_map/ppermute | solution.py:412
  120.1 5.0 %collective-permute-start.36 = (bf16[1024,256]{1,0:T(8,128)(2,1)S(1)}, bf16[1024,256]{1,0:T(8,128)(2,1)S(1)}, u32[]{:S(2)}, u32[]{:S(2)}) collective-permute-start(bf16[1024,256]{1,0:T(8,128)(2,1)S(1)} %collective-permute-done.35.refs_9_.refs_3_), channel_id=1, source_target_pairs={{0,16},{16,0},{1,17},{17,1},{2,18},{18,2},{3,19},{19,3},{4,20},{20... | collective-permute-start | bytes 1572872 | tf_op jit(solution)/shard_map/ppermute | solution.py:412
  125.0 7.7 %collective-permute-start.32 = (bf16[512,256]{1,0:T(8,128)(2,1)S(1)}, bf16[512,256]{1,0:T(8,128)(2,1)S(1)}, u32[]{:S(2)}, u32[]{:S(2)}) collective-permute-start(bf16[512,256]{1,0:T(8,128)(2,1)S(1)} %broadcast_select_fusion), channel_id=1, source_target_pairs={{0,1},{1,2},{2,3},{3,4},{4,5},{5,6},{6,7},{7,0},{16,23},{17,16},{1... | collective-permute-start | bytes 786440 | tf_op jit(solution)/shard_map/ppermute | solution.py:38
  133.6 8.8 %collective-permute-start.37 = (bf16[512,256]{1,0:T(8,128)(2,1)S(1)}, bf16[512,256]{1,0:T(8,128)(2,1)S(1)}, u32[]{:S(2)}, u32[]{:S(2)}) collective-permute-start(bf16[512,256]{1,0:T(8,128)(2,1)S(1)} %get-tuple-element.26), channel_id=1, source_target_pairs={{0,8},{8,0},{1,9},{9,1},{2,10},{10,2},{3,11},{11,3},{4,12},{12,4},... | collective-permute-start | bytes 786440 | tf_op jit(solution)/shard_map/ppermute | solution.py:416
where the time goes:
time: 144 us; the launch traced here: 143 us
  starting transfers between devices  59.3 us (41%)
  waiting for transfers between devices  46.3 us (32%)
  Pallas kernels  24 us (17%)
  local copies, waits for them, and re-layouts  7.23 us (5%)
  other arithmetic  5.96 us (4%)
    ppermute x18, starting transfers between devices, shift(): return lax.ppermute(x, axis, [(i, (i + by) % size) for i in range(size)])  28.9 us
    ppermute x18, waiting for transfers between devices, shift(): return lax.ppermute(x, axis, [(i, (i + by) % size) for i in range(size)])  19.8 us
    pallas_call x3, Pallas kernels, attend(): pl.pallas_call(functools.partial(attend_kernel, which, before is None, fi...  13.8 us
    ppermute x2, waiting for transfers between devices, ring(): lax.ppermute(last, ('core', 'z'), pairs)  10.4 us
    ppermute x1, starting transfers between devices, shards(): kv_got = lax.ppermute(kv_send, 'xl', SWAP)  9.32 us
    ppermute x2, starting transfers between devices, shards(): qw = [lax.ppermute(qw_in, chip_x, t) for t in (TAKE_0, TAKE_1)]  5.54 us
    pallas_call x2, Pallas kernels, project_most(): pl.pallas_call(functools.partial(proj_kernel, 'most', with_squares, n_w,...  4.89 us
    ppermute x1, waiting for transfers between devices, shards(): kv_x = lax.ppermute(kv, 'xh', SWAP)  4.85 us
  transfers between devices with their start and end apart: 38, of which 14 were waited for; matrix products, arithmetic and copies ran while one was open for 8% of the time, Pallas kernels for 14%

commit v1 on v0

--- a/solution.py
+++ b/solution.py
@@ -209,19 +209,23 @@
     )(scal, *xs, last, *ws)
 
 
-PROJECT_VMEM = 20 << 20
-ATTEND_VMEM = 28 << 20
-
-
-def attend_kernel(which, first, final, scal, coef_ref, q_ref, q_other_ref, *refs):
+PROJECT_VMEM = 10 << 20
+ATTEND_VMEM = 16 << 20
+
+
+def attend_kernel(which, first, final, scal, *refs):
     n = len(which)
+    if first:
+        coef_ref, q_ref, q_other_ref, *refs = refs
+    else:
+        q_scr, before, *refs = refs
     kvs, refs = refs[:n], refs[n:]
-    if not first:
-        before, refs = refs[0], refs[1:]
-    if final:
-        own_out, other_out, k_scr, v_scr, q_scr, acc = refs
+    if first:
+        acc, q_scr, k_scr, v_scr = refs
+    elif final:
+        own_out, other_out, k_scr, v_scr, acc = refs
     else:
-        acc, k_scr, v_scr, q_scr = refs
+        acc, k_scr, v_scr = refs
     rows = acc.shape[1]
 
     def one_hot(ref, at):
@@ -243,14 +247,14 @@
         for at in range(0, rows, 256):
             k_scr[i, at : at + 256, HD:] = one_hot(kvs[i], at).astype(BF)
         v_scr[i] = kvs[i][:rows, HD:]
-    for g, ref in enumerate((q_ref, q_other_ref)):
-        for at in range(0, rows, 256):
-            hot = one_hot(ref, at)
+    if first:
+        for g, ref in enumerate((q_ref, q_other_ref)):
+            for at in range(0, rows, 256):
+                hot = one_hot(ref, at)
+                for h in range(2):
+                    q_scr[g, h, at : at + 256, HD:] = (hot * coef_ref[h : h + 1, :]).astype(BF)
             for h in range(2):
-                q_scr[g, h, at : at + 256, HD:] = (hot * coef_ref[h : h + 1, :]).astype(BF)
-        for h in range(2):
-            q_scr[g, h, :, :HD] = ref[:rows, h * HD : (h + 1) * HD]
-    if first:
+                q_scr[g, h, :, :HD] = ref[:rows, h * HD : (h + 1) * HD]
         acc[...] = jnp.zeros_like(acc)
     else:
         acc[...] = before[...]
@@ -281,11 +285,10 @@
 
         def one(k, carry):
             g, i = k // n, lax.rem(k, n)
-            own = k == 0
-
-            @pl.when(jnp.logical_or(own, place_of(i) < scal[4 + g]))
+
+            @pl.when(jnp.logical_or(k == 0, place_of(i) < scal[4 + g]))
             def _():
-                tile(g, i, jnp.where(own, 0, rows))
+                tile(g, i, jnp.where(k == 0, 0, rows))
 
             return carry
 
@@ -306,27 +309,25 @@
         other_out[...] = acc[1].astype(BF)
 
 
-def attend(scal, coef, q, q_other, kvs, which, before=None, final=False):
-    rows = q.shape[0] - 16
+def attend(scal, queries, kvs, which, before=None, final=False):
+    rows = kvs[0].shape[0] - 16
     n = len(kvs)
-    sums = jax.ShapeDtypeStruct((2, rows, 2 * HD), F32)
-    out = [sums]
-    scratch = [
-        pltpu.VMEM((n, rows, 2 * HD), BF),
-        pltpu.VMEM((n, rows, HD), BF),
-        pltpu.VMEM((2, 2, rows, 2 * HD), BF),
-    ]
+    first = before is None
+    out = [jax.ShapeDtypeStruct((2, rows, 2 * HD), F32)]
+    scratch = [pltpu.VMEM((n, rows, 2 * HD), BF), pltpu.VMEM((n, rows, HD), BF)]
+    if first:
+        out.append(jax.ShapeDtypeStruct((2, 2, rows, 2 * HD), BF))
     if final:
         out = [
             jax.ShapeDtypeStruct((rows, 2 * HD), F32),
             jax.ShapeDtypeStruct((rows, 2 * HD), BF),
         ]
         scratch.append(pltpu.VMEM((2, rows, 2 * HD), F32))
-    extra = [] if before is None else [before]
+    ins = [*queries] if first else [*queries, before]
     return pl.pallas_call(
-        functools.partial(attend_kernel, which, before is None, final),
+        functools.partial(attend_kernel, which, first, final),
         out_shape=out,
-        in_specs=[SM] + [VM] * (3 + n + len(extra)),
+        in_specs=[SM] + [VM] * (len(ins) + n),
         out_specs=[VM] * len(out),
         scratch_shapes=scratch,
         cost_estimate=pl.CostEstimate(
@@ -334,7 +335,7 @@
         ),
         compiler_params=pltpu.CompilerParams(vmem_limit_bytes=ATTEND_VMEM),
         name="attend",
-    )(scal, coef, q, q_other, *kvs, *extra)
+    )(scal, *ins, *kvs)
 
 
 def shards(events, domain_ids, block_order, query_weight, keyval_weight, head_bias, out_weight):
@@ -391,7 +392,7 @@
     kv_x_down = shift(kv_x, "y", NY, -1)
     kv_x_far = shift(kv_x_down, "y", NY, -1)
 
-    qw = jnp.concatenate(qw, axis=1)
+    qw = jnp.concatenate(lax.optimization_barrier((*qw, kv_send))[:2], axis=1)
     q_w = [qw, lax.ppermute(qw, "y", [(i, i ^ 1) for i in range(NY)])]
     q_w += [lax.ppermute(w, "core", SWAP) for w in q_w]
     q_keep, q_send = project_all(scal, 3, xs, last, q_w)
@@ -402,9 +403,10 @@
 
     ow = [lax.ppermute(out_weight, chip_x, t) for t in (TAKE_0, TAKE_1)]
 
-    part = attend(scal, coef, q, q_other, [kv, kv_up, kv_down], (0, 2, 4))[0]
-    part = attend(scal, coef, q, q_other, [kv_x, kv_far, kv_x_up, kv_x_down], (1, 6, 3, 5), part)[0]
-    mine, theirs = attend(scal, coef, q, q_other, [kv_x_far], (7,), part, True)
+    part, full = attend(scal, (coef, q, q_other), [kv, kv_up, kv_down], (0, 2, 4))
+    rest = [kv_x, kv_far, kv_x_up, kv_x_down]
+    part = attend(scal, (full,), rest, (1, 6, 3, 5), part)[0]
+    mine, theirs = attend(scal, (full,), [kv_x_far], (7,), part, True)
     back = lax.ppermute(theirs, "core", SWAP)
     attended = ((mine + back.astype(F32)) * inv).astype(BF)
 

time: 144 us -> 150 us (1.042)
  waiting for transfers between devices: 46.3 us -> 61.3 us
  starting transfers between devices: 59.3 us -> 52.1 us
    ppermute x1, waiting for transfers between devices: 0.01 us -> 10.3 us  [shards(): q_w = [qw, lax.ppermute(qw, 'y', [(i, i ^ 1) for i in range(NY)])]]
    ppermute x1, starting transfers between devices: 9.32 us -> 2.91 us  [shards(): kv_got = lax.ppermute(kv_send, 'xl', SWAP)]
    ppermute x1, waiting for transfers between devices: 0.01 us -> 4.72 us  [shards(): other = lax.ppermute(mine, 'z', [(i, i ^ 1) for i in range(NZ)])]
    ppermute x18, waiting for transfers between devices: 19.8 us -> 23.4 us  [shift(): return lax.ppermute(x, axis, [(i, (i + by) % size) for i in range(size)])]
    ppermute x1, waiting for transfers between devices: 4.85 us -> 2.25 us  [shards(): kv_x = lax.ppermute(kv, 'xh', SWAP)]
    ppermute x1, waiting for transfers between devices: 2.47 us -> 0.49 us  [shards(): kv_got = lax.ppermute(kv_send, 'xl', SWAP)]
  transfers between devices with their start and end apart: 38 -> 38, of which waited for: 14 -> 16; matrix products, arithmetic and copies ran while one was open for 8% -> 7% of each run, Pallas kernels for 14% -> 13%
where the time goes in v1:
time: 150 us; the launch traced here: 149 us
  waiting for transfers between devices  61.3 us (41%)
  starting transfers between devices  52.1 us (35%)
  Pallas kernels  23.2 us (15%)
  local copies, waits for them, and re-layouts  6.53 us (4%)
  other arithmetic  5.43 us (4%)
    ppermute x18, starting transfers between devices, shift(): return lax.ppermute(x, axis, [(i, (i + by) % size) for i in range(size)])  28.1 us
    ppermute x18, waiting for transfers between devices, shift(): return lax.ppermute(x, axis, [(i, (i + by) % size) for i in range(size)])  23.4 us
    pallas_call x3, Pallas kernels, attend(): pl.pallas_call(functools.partial(attend_kernel, which, first, final), out...  13.5 us
    ppermute x2, waiting for transfers between devices, ring(): lax.ppermute(last, ('core', 'z'), pairs)  10.8 us
    ppermute x1, waiting for transfers between devices, shards(): q_w = [qw, lax.ppermute(qw, 'y', [(i, i ^ 1) for i in range(NY)])]  10.3 us
    ppermute x2, starting transfers between devices, shards(): qw = [lax.ppermute(qw_in, chip_x, t) for t in (TAKE_0, TAKE_1)]  5.54 us
    ppermute x1, starting transfers between devices, shards(): o_got = lax.ppermute(o_send, 'xl', SWAP)  5.26 us
    ppermute x2, starting transfers between devices, shards(): ow = [lax.ppermute(out_weight, chip_x, t) for t in (TAKE_0, TAKE_1)]  4.95 us
  transfers between devices with their start and end apart: 38, of which 16 were waited for; matrix products, arithmetic and copies ran while one was open for 7% of the time, Pallas kernels for 13%

profile of v1, /device:TPU:8, one launch (start us, length us, event | category | flops | bytes accessed | tf_op | source)
XLA Modules:
  0.0 149.0 jit_solution(3443259286823428719)
XLA Ops:
  0.0 2.0 %collective-permute-start = (bf16[512,256]{1,0:T(8,128)(2,1)}, bf16[512,256]{1,0:T(8,128)(2,1)S(1)}, u32[]{:S(2)}, u32[]{:S(2)}) collective-permute-start(bf16[512,256]{1,0:T(8,128)(2,1)} %refs_0_.3), channel_id=1, source_target_pairs={{0,1},{1,2},{2,3},{3,4},{4,5},{5,6},{6,7},{7,0},{8,9},{9,10},{10,1... | collective-permute-start | bytes 786440 | tf_op jit(solution)/shard_map/ppermute | solution.py:27
  2.0 4.0 %collective-permute-start.3 = (bf16[512,256]{1,0:T(8,128)(2,1)}, bf16[512,256]{1,0:T(8,128)(2,1)S(1)}, u32[]{:S(2)}, u32[]{:S(2)}) collective-permute-start(bf16[512,256]{1,0:T(8,128)(2,1)} %refs_0_.3), channel_id=1, source_target_pairs={{0,7},{1,0},{2,1},{3,2},{4,3},{5,4},{6,5},{7,6},{8,15},{9,8},{10,9... | collective-permute-start | bytes 786440 | tf_op jit(solution)/shard_map/ppermute | solution.py:27
  6.1 2.3 %constant_dynamic-slice_fusion.1 = (bf16[1024,1,1,128]{3,2,1,0:T(2,128)(2,1)S(1)}, bf16[1024,1,1,128]{3,2,1,0:T(2,128)(2,1)S(1)}) fusion(bf16[1024,8,2,128]{3,2,1,0:T(2,128)(2,1)} %param.13, s32[]{:T(128)S(6)} %select_n.86, s32[]{:T(128)S(6)} %select_n.88, s32[]{:T(128)S(6)} %select_n.89), kind=kLoop, calls=%fused_computation.26 | loop fusion | bytes 1048588 | tf_op jit(solution)/shard_map/dynamic_slice | solution.py:349
  8.5 0.7 collective-permute-start.9
  9.2 3.3 %collective-permute-done.refs_1_ = bf16[512,256]{1,0:T(8,128)(2,1)S(1)} collective-permute-done((bf16[512,256]{1,0:T(8,128)(2,1)}, bf16[512,256]{1,0:T(8,128)(2,1)S(1)}, u32[]{:S(2)}, u32[]{:S(2)}) %collective-permute-start) | collective-permute-done | bytes 262176 | tf_op jit(solution)/shard_map/ppermute | solution.py:27
  12.5 3.2 %collective-permute-start.4 = (bf16[512,256]{1,0:T(8,128)(2,1)S(1)}, bf16[512,256]{1,0:T(8,128)(2,1)S(1)}, u32[]{:S(2)}, u32[]{:S(2)}) collective-permute-start(bf16[512,256]{1,0:T(8,128)(2,1)S(1)} %collective-permute-done.3.refs_6_), channel_id=1, source_target_pairs={{0,7},{1,0},{2,1},{3,2},{4,3},{5,4},{6,5},{7,6},{8,15},{9,8},{10,9... | collective-permute-start | bytes 786440 | tf_op jit(solution)/shard_map/ppermute | solution.py:27
  15.7 0.7 constant_dynamic-slice_fusion.2
  16.4 3.6 %collective-permute-start.7 = (bf16[512,256]{1,0:T(8,128)(2,1)}, bf16[512,256]{1,0:T(8,128)(2,1)}, u32[]{:S(2)}, u32[]{:S(2)}) collective-permute-start(bf16[512,256]{1,0:T(8,128)(2,1)} %constant_dynamic-slice_fusion.2), channel_id=1, source_target_pairs={{0,0},{32,8},{8,32},{40,40},{1,1},{33,9},{9,33},{41,41},{2,2},{34,... | collective-permute-start | bytes 786440 | tf_op jit(solution)/shard_map/ppermute | solution.py:357
  20.0 2.0 %collective-permute-start.8 = (bf16[512,256]{1,0:T(8,128)(2,1)}, bf16[512,256]{1,0:T(8,128)(2,1)}, u32[]{:S(2)}, u32[]{:S(2)}) collective-permute-start(bf16[512,256]{1,0:T(8,128)(2,1)} %constant_dynamic-slice_fusion.2), channel_id=1, source_target_pairs={{8,0},{40,8},{0,32},{32,40},{9,1},{41,9},{1,33},{33,41},{10,2},{42... | collective-permute-start | bytes 786440 | tf_op jit(solution)/shard_map/ppermute | solution.py:357
  22.0 3.2 %collective-permute-start.5 = (bf16[512,256]{1,0:T(8,128)(2,1)S(1)}, bf16[512,256]{1,0:T(8,128)(2,1)S(1)}, u32[]{:S(2)}, u32[]{:S(2)}) collective-permute-start(bf16[512,256]{1,0:T(8,128)(2,1)S(1)} %collective-permute-done.4.refs_5_), channel_id=1, source_target_pairs={{0,7},{1,0},{2,1},{3,2},{4,3},{5,4},{6,5},{7,6},{8,15},{9,8},{10,9... | collective-permute-start | bytes 786440 | tf_op jit(solution)/shard_map/ppermute | solution.py:27
  25.5 4.1 %collective-permute-done.2.refs_3_ = bf16[512,256]{1,0:T(8,128)(2,1)S(1)} collective-permute-done((bf16[512,256]{1,0:T(8,128)(2,1)S(1)}, bf16[512,256]{1,0:T(8,128)(2,1)S(1)}, u32[]{:S(2)}, u32[]{:S(2)}) %collective-permute-start.2) | collective-permute-done | bytes 262176 | tf_op jit(solution)/shard_map/ppermute | solution.py:27
  29.6 0.7 broadcast_select_fusion.1
  30.4 0.1 concatenate.18.scal
  30.5 2.4 %project_most.2 = (f32[512,256]{1,0:T(8,128)S(1)}, f32[8,512]{1,0:T(8,128)S(1)}) custom-call(s32[15]{0:T(128)S(1)} %concatenate.18.scal, bf16[512,256]{1,0:T(8,128)(2,1)S(1)} %copy-done.1, bf16[512,256]{1,0:T(8,128)(2,1)S(1)} %collective-permute-done.refs_1_, bf16[512,256]{1,0:T(8,128)(2,1)S(1)} %collective-permute-done.1.refs_2_, ...), custom_call_target="tpu_custom_call" | custom-call | flops 469762048 | bytes 1048576 | tf_op jit(solution)/shard_map/project_most/pallas_call | solution.py:153
  32.9 5.4 %collective-permute-done.6.refs_0_.refs_7_ = bf16[512,256]{1,0:T(8,128)(2,1)} collective-permute-done((bf16[512,256]{1,0:T(8,128)(2,1)}, bf16[512,256]{1,0:T(8,128)(2,1)}, u32[]{:S(2)}, u32[]{:S(2)}) %collective-permute-start.6) | collective-permute-done | bytes 262176 | tf_op jit(solution)/shard_map/ppermute | solution.py:38
  38.2 1.5 %project_last.2 = (f32[512,128]{1,0:T(8,128)S(1)}, bf16[528,128]{1,0:T(8,128)(2,1)S(1)}, f32[8,512]{1,0:T(8,128)S(1)}) custom-call(s32[15]{0:T(128)S(1)} %concatenate.18.scal, bf16[512,256]{1,0:T(8,128)(2,1)} %collective-permute-done.6.refs_0_.refs_7_, bf16[1024,256]{1,0:T(8,128)(2,1)S(1)} %collective-permute-done.9.refs_7_.refs_1_, ...), custom_call_target="tpu_custom_call" | custom-call | tf_op jit(solution)/shard_map/project_last/pallas_call | solution.py:180
  39.8 2.9 %collective-permute-start.15 = (bf16[528,128]{1,0:T(8,128)(2,1)S(1)}, bf16[528,128]{1,0:T(8,128)(2,1)S(1)}, u32[]{:S(2)}, u32[]{:S(2)}) collective-permute-start(bf16[528,128]{1,0:T(8,128)(2,1)S(1)} %get-tuple-element.22), channel_id=1, source_target_pairs={{0,8},{8,0},{1,9},{9,1},{2,10},{10,2},{3,11},{11,3},{4,12},{12,4},... | collective-permute-start | bytes 405512 | tf_op jit(solution)/shard_map/ppermute | solution.py:379
  42.7 1.0 constant_dynamic-update-slice_fusion.1
  43.6 1.0 constant_dynamic-update-slice_fusion.refs_8_
  44.6 0.5 collective-permute-start.11
  45.2 0.5 collective-permute-done.15
  45.7 0.7 copy-done.3
  46.4 10.3 %collective-permute-done.11.refs_9_ = bf16[512,512]{1,0:T(8,128)(2,1)S(1)} collective-permute-done((bf16[512,512]{1,0:T(8,128)(2,1)S(1)}, bf16[512,512]{1,0:T(8,128)(2,1)S(1)}, u32[]{:S(2)}, u32[]{:S(2)}) %collective-permute-start.11) | collective-permute-done | bytes 524320 | tf_op jit(solution)/shard_map/ppermute | solution.py:396
  56.7 1.1 multiply_convert_fusion.2
  57.9 0.6 convert_element_type.39
  58.5 0.7 reshape.52
  59.2 4.7 %collective-permute-done.17 = bf16[512,128]{1,0:T(8,128)(2,1)} collective-permute-done((bf16[512,128]{1,0:T(8,128)(2,1)S(1)}, bf16[512,128]{1,0:T(8,128)(2,1)}, u32[]{:S(2)}, u32[]{:S(2)}) %collective-permute-start.17) | collective-permute-done | bytes 131104 | tf_op jit(solution)/shard_map/ppermute | solution.py:383
  63.9 0.9 broadcast_select_fusion.3
  64.9 1.9 %collective-permute-start.20 = (bf16[528,256]{1,0:T(8,128)(2,1)S(1)}, bf16[528,256]{1,0:T(8,128)(2,1)S(1)}, u32[]{:S(2)}, u32[]{:S(2)}) collective-permute-start(bf16[528,256]{1,0:T(8,128)(2,1)S(1)} %pad_maximum_fusion.2.refs_3_), channel_id=1, source_target_pairs={{0,32},{32,0},{1,33},{33,1},{2,34},{34,2},{3,35},{35,3},{4,36},{36... | collective-permute-start | bytes 811016 | tf_op jit(solution)/shard_map/ppermute | solution.py:387
  66.8 2.8 %project_all.1 = (f32[512,256]{1,0:T(8,128)S(1)}, bf16[512,256]{1,0:T(8,128)(2,1)S(1)}) custom-call(s32[15]{0:T(128)S(1)} %concatenate.18.scal, bf16[512,256]{1,0:T(8,128)(2,1)S(1)} %copy-done.1, bf16[512,256]{1,0:T(8,128)(2,1)S(1)} %collective-permute-done.refs_1_, bf16[512,256]{1,0:T(8,128)(2,1)S(1)} %collective-permute-done.1.refs_2_, ...), custom_call_target="tpu_custom_call" | custom-call | flops 1073741824 | bytes 2097152 | tf_op jit(solution)/shard_map/project_all/pallas_call | solution.py:198
  69.7 1.2 collective-permute-start.14
  70.9 0.7 multiply_subtract_fusion
  71.6 1.6 %collective-permute-start.18 = (bf16[528,256]{1,0:T(8,128)(2,1)S(1)}, bf16[528,256]{1,0:T(8,128)(2,1)S(1)}, u32[]{:S(2)}, u32[]{:S(2)}) collective-permute-start(bf16[528,256]{1,0:T(8,128)(2,1)S(1)} %pad_maximum_fusion.2.refs_3_), channel_id=1, source_target_pairs={{0,64},{64,128},{128,192},{192,0},{1,65},{65,129},{129,193},{193,1... | collective-permute-start | bytes 811016 | tf_op jit(solution)/shard_map/ppermute | solution.py:27
  73.1 0.5 collective-permute-start.19
  73.6 2.2 %collective-permute-done.20.refs_2_ = bf16[528,256]{1,0:T(8,128)(2,1)S(1)} collective-permute-done((bf16[528,256]{1,0:T(8,128)(2,1)S(1)}, bf16[528,256]{1,0:T(8,128)(2,1)S(1)}, u32[]{:S(2)}, u32[]{:S(2)}) %collective-permute-start.20) | collective-permute-done | bytes 270368 | tf_op jit(solution)/shard_map/ppermute | solution.py:387
  75.8 0.5 collective-permute-start.23
  76.3 3.3 %collective-permute-done.14 = bf16[512,256]{1,0:T(8,128)(2,1)S(1)} collective-permute-done((bf16[512,256]{1,0:T(8,128)(2,1)S(1)}, bf16[512,256]{1,0:T(8,128)(2,1)S(1)}, u32[]{:S(2)}, u32[]{:S(2)}) %collective-permute-start.14) | collective-permute-done | bytes 262176 | tf_op jit(solution)/shard_map/ppermute | solution.py:399
  79.6 0.1 multiply_convert_fusion.1
  79.9 1.6 %collective-permute-start.22 = (bf16[528,256]{1,0:T(8,128)(2,1)S(1)}, bf16[528,256]{1,0:T(8,128)(2,1)S(1)}, u32[]{:S(2)}, u32[]{:S(2)}) collective-permute-start(bf16[528,256]{1,0:T(8,128)(2,1)S(1)} %collective-permute-done.20.refs_2_), channel_id=1, source_target_pairs={{0,64},{64,128},{128,192},{192,0},{1,65},{65,129},{129,193},{193,1... | collective-permute-start | bytes 811016 | tf_op jit(solution)/shard_map/ppermute | solution.py:27
  81.5 1.3 collective-permute-start.21
  82.8 3.3 %collective-permute-done.23.refs_5_ = bf16[528,256]{1,0:T(8,128)(2,1)S(1)} collective-permute-done((bf16[528,256]{1,0:T(8,128)(2,1)S(1)}, bf16[528,256]{1,0:T(8,128)(2,1)S(1)}, u32[]{:S(2)}, u32[]{:S(2)}) %collective-permute-start.23) | collective-permute-done | bytes 270368 | tf_op jit(solution)/shard_map/ppermute | solution.py:27
  86.1 0.5 collective-permute-start.24
  86.6 6.2 %attend.3 = (f32[2,512,256]{2,1,0:T(8,128)S(1)}, bf16[2,2,512,256]{3,2,1,0:T(8,128)(2,1)S(1)}) custom-call(s32[15]{0:T(128)S(1)} %concatenate.18.scal, f32[2,128]{1,0:T(2,128)S(1)} %select_select_fusion.refs_0_, bf16[528,256]{1,0:T(8,128)(2,1)S(1)} %pad_maximum_fusion.1.refs_1_, bf16[528,256]{1,0:T(8,128)(2,1)S(1)} %collective-permute-done.16.refs_2_, ...), custom_call_target="tpu_custom_call" | custom-call | flops 3221225472 | bytes 1048576 | tf_op jit(solution)/shard_map/attend/pallas_call | solution.py:327
  92.8 1.8 %collective-permute-done.21.refs_3_ = bf16[528,256]{1,0:T(8,128)(2,1)S(1)} collective-permute-done((bf16[528,256]{1,0:T(8,128)(2,1)S(1)}, bf16[528,256]{1,0:T(8,128)(2,1)S(1)}, u32[]{:S(2)}, u32[]{:S(2)}) %collective-permute-start.21) | collective-permute-done | bytes 270368 | tf_op jit(solution)/shard_map/ppermute | solution.py:27
  94.6 4.9 %attend.4.refs_1_ = f32[2,512,256]{2,1,0:T(8,128)S(1)} custom-call(s32[15]{0:T(128)S(1)} %concatenate.18.scal, bf16[2,2,512,256]{3,2,1,0:T(8,128)(2,1)S(1)} %get-tuple-element.29.refs_0_, f32[2,512,256]{2,1,0:T(8,128)S(1)} %get-tuple-element.30.refs_1_, bf16[528,256]{1,0:T(8,128)(2,1)S(1)} %collective-permute-done.20.refs_2_, ...), custom_call_target="tpu_custom_call" | custom-call | flops 4294967296 | bytes 1048576 | tf_op jit(solution)/shard_map/attend/pallas_call | solution.py:327
  99.6 2.4 %attend.5 = (f32[512,256]{1,0:T(8,128)S(1)}, bf16[512,256]{1,0:T(8,128)(2,1)S(1)}) custom-call(s32[15]{0:T(128)S(1)} %concatenate.18.scal, bf16[2,2,512,256]{3,2,1,0:T(8,128)(2,1)S(1)} %get-tuple-element.29.refs_0_, f32[2,512,256]{2,1,0:T(8,128)S(1)} %attend.4.refs_1_, bf16[528,256]{1,0:T(8,128)(2,1)S(1)} %collective-permute-done.24.refs_2_), custom_call_target="tpu_custom_call" | custom-call | flops 1073741824 | bytes 1048576 | tf_op jit(solution)/shard_map/attend/pallas_call | solution.py:327
  102.1 1.5 collective-permute-done.25
  103.5 0.1 multiply_convert_fusion.refs_0_
  103.7 0.6 collective-permute-start.26
  104.3 2.7 %collective-permute-start.29 = (bf16[512,256]{1,0:T(8,128)(2,1)S(1)}, bf16[512,256]{1,0:T(8,128)(2,1)S(1)}, u32[]{:S(2)}, u32[]{:S(2)}) collective-permute-start(bf16[512,256]{1,0:T(8,128)(2,1)S(1)} %multiply_convert_fusion.refs_0_), channel_id=1, source_target_pairs={{0,7},{1,0},{2,1},{3,2},{4,3},{5,4},{6,5},{7,6},{8,15},{9,8},{10,9... | collective-permute-start | bytes 786440 | tf_op jit(solution)/shard_map/ppermute | solution.py:27
  107.0 0.7 collective-permute-start.33
  107.7 4.3 %collective-permute-start.35 = (bf16[1024,256]{1,0:T(8,128)(2,1)S(1)}, bf16[1024,256]{1,0:T(8,128)(2,1)S(1)}, u32[]{:S(2)}, u32[]{:S(2)}) collective-permute-start(bf16[1024,256]{1,0:T(8,128)(2,1)S(1)} %copy-done.6), channel_id=1, source_target_pairs={{8,0},{40,8},{0,32},{32,40},{9,1},{41,9},{1,33},{33,41},{10,2},{42... | collective-permute-start | bytes 1572872 | tf_op jit(solution)/shard_map/ppermute | solution.py:404
  112.0 1.4 collective-permute-done.26.refs_1_
  113.3 3.2 %collective-permute-start.30 = (bf16[512,256]{1,0:T(8,128)(2,1)S(1)}, bf16[512,256]{1,0:T(8,128)(2,1)S(1)}, u32[]{:S(2)}, u32[]{:S(2)}) collective-permute-start(bf16[512,256]{1,0:T(8,128)(2,1)S(1)} %collective-permute-done.29.refs_6_), channel_id=1, source_target_pairs={{0,7},{1,0},{2,1},{3,2},{4,3},{5,4},{6,5},{7,6},{8,15},{9,8},{10,9... | collective-permute-start | bytes 786440 | tf_op jit(solution)/shard_map/ppermute | solution.py:27
  116.6 5.5 %collective-permute-done.27.refs_2_ = bf16[512,256]{1,0:T(8,128)(2,1)S(1)} collective-permute-done((bf16[512,256]{1,0:T(8,128)(2,1)S(1)}, bf16[512,256]{1,0:T(8,128)(2,1)S(1)}, u32[]{:S(2)}, u32[]{:S(2)}) %collective-permute-start.27) | collective-permute-done | bytes 262176 | tf_op jit(solution)/shard_map/ppermute | solution.py:27
  122.0 3.2 %collective-permute-start.31 = (bf16[512,256]{1,0:T(8,128)(2,1)S(1)}, bf16[512,256]{1,0:T(8,128)(2,1)S(1)}, u32[]{:S(2)}, u32[]{:S(2)}) collective-permute-start(bf16[512,256]{1,0:T(8,128)(2,1)S(1)} %collective-permute-done.30.refs_5_), channel_id=1, source_target_pairs={{0,7},{1,0},{2,1},{3,2},{4,3},{5,4},{6,5},{7,6},{8,15},{9,8},{10,9... | collective-permute-start | bytes 786440 | tf_op jit(solution)/shard_map/ppermute | solution.py:27
  125.3 0.5 collective-permute-start.36
  125.8 4.1 %collective-permute-done.28.refs_3_ = bf16[512,256]{1,0:T(8,128)(2,1)S(1)} collective-permute-done((bf16[512,256]{1,0:T(8,128)(2,1)S(1)}, bf16[512,256]{1,0:T(8,128)(2,1)S(1)}, u32[]{:S(2)}, u32[]{:S(2)}) %collective-permute-start.28) | collective-permute-done | bytes 262176 | tf_op jit(solution)/shard_map/ppermute | solution.py:27
  130.0 2.0 %project_most.3.refs_5_ = f32[512,512]{1,0:T(8,128)S(1)} custom-call(s32[15]{0:T(128)S(1)} %concatenate.18.scal, bf16[512,256]{1,0:T(8,128)(2,1)S(1)} %multiply_convert_fusion.refs_0_, bf16[512,256]{1,0:T(8,128)(2,1)S(1)} %collective-permute-done.26.refs_1_, bf16[512,256]{1,0:T(8,128)(2,1)S(1)} %collective-permute-done.27.refs_2_, ...), custom_call_target="tpu_custom_call" | custom-call | flops 939524096 | bytes 2097152 | tf_op jit(solution)/shard_map/project_most/pallas_call | solution.py:153
  132.1 5.5 %collective-permute-done.32.refs_0_ = bf16[512,256]{1,0:T(8,128)(2,1)S(1)} collective-permute-done((bf16[512,256]{1,0:T(8,128)(2,1)S(1)}, bf16[512,256]{1,0:T(8,128)(2,1)S(1)}, u32[]{:S(2)}, u32[]{:S(2)}) %collective-permute-start.32) | collective-permute-done | bytes 262176 | tf_op jit(solution)/shard_map/ppermute | solution.py:38
  137.6 0.9 project_last.3
  138.5 5.3 %collective-permute-start.37 = (bf16[512,256]{1,0:T(8,128)(2,1)S(1)}, bf16[512,256]{1,0:T(8,128)(2,1)S(1)}, u32[]{:S(2)}, u32[]{:S(2)}) collective-permute-start(bf16[512,256]{1,0:T(8,128)(2,1)S(1)} %get-tuple-element.34), channel_id=1, source_target_pairs={{0,8},{8,0},{1,9},{9,1},{2,10},{10,2},{3,11},{11,3},{4,12},{12,4},... | collective-permute-start | bytes 786440 | tf_op jit(solution)/shard_map/ppermute | solution.py:418
  143.8 4.4 %collective-permute-done.37 = bf16[512,256]{1,0:T(8,128)(2,1)S(1)} collective-permute-done((bf16[512,256]{1,0:T(8,128)(2,1)S(1)}, bf16[512,256]{1,0:T(8,128)(2,1)S(1)}, u32[]{:S(2)}, u32[]{:S(2)}) %collective-permute-start.37) | collective-permute-done | bytes 262176 | tf_op jit(solution)/shard_map/ppermute | solution.py:418
  148.2 0.8 add_convert_fusion
  (69 shorter events, 1.0 us)
Async XLA Ops:
  0.0 15.7 %copy-start = (bf16[1024,256]{1,0:T(8,128)(2,1)S(1)}, bf16[1024,256]{1,0:T(8,128)(2,1)}, u32[]{:S(2)}) copy-start(bf16[1024,256]{1,0:T(8,128)(2,1)} %param.12) | copy-start | bytes 1572868
  0.0 25.2 %copy-start.8 = (s32[8]{0:T(128)S(1)}, s32[8]{0:T(128)}, u32[]{:S(2)}) copy-start(s32[8]{0:T(128)} %constant.112) | copy-start | bytes 100
  0.0 30.3 %copy-start.5 = (s32[8]{0:T(128)S(1)}, s32[8]{0:T(128)}, u32[]{:S(2)}) copy-start(s32[8]{0:T(128)} %constant.108.clone) | copy-start | bytes 100
  0.0 30.5 %copy-start.1 = (bf16[512,256]{1,0:T(8,128)(2,1)S(1)}, bf16[512,256]{1,0:T(8,128)(2,1)}, u32[]{:S(2)}) copy-start(bf16[512,256]{1,0:T(8,128)(2,1)} %refs_0_.3) | copy-start | bytes 786436
  0.0 25.3 %copy-start.7 = (s32[4]{0:T(128)S(1)}, s32[4]{0:T(128)}, u32[]{:S(2)}) copy-start(s32[4]{0:T(128)} %param.11) | copy-start | bytes 52
  0.0 12.4 %collective-permute-start = (bf16[512,256]{1,0:T(8,128)(2,1)}, bf16[512,256]{1,0:T(8,128)(2,1)S(1)}, u32[]{:S(2)}, u32[]{:S(2)}) collective-permute-start(bf16[512,256]{1,0:T(8,128)(2,1)} %refs_0_.3), channel_id=1, source_target_pairs={{0,1},{1,2},{2,3},{3,4},{4,5},{5,6},{6,7},{7,0},{8,9},{9,10},{10,1... | collective-permute-start | bytes 786440 | tf_op jit(solution)/shard_map/ppermute | solution.py:27
  2.0 10.5 %collective-permute-start.3 = (bf16[512,256]{1,0:T(8,128)(2,1)}, bf16[512,256]{1,0:T(8,128)(2,1)S(1)}, u32[]{:S(2)}, u32[]{:S(2)}) collective-permute-start(bf16[512,256]{1,0:T(8,128)(2,1)} %refs_0_.3), channel_id=1, source_target_pairs={{0,7},{1,0},{2,1},{3,2},{4,3},{5,4},{6,5},{7,6},{8,15},{9,8},{10,9... | collective-permute-start | bytes 786440 | tf_op jit(solution)/shard_map/ppermute | solution.py:27
  8.4 49.5 %copy-start.4 = (s32[512]{0:T(512)S(1)}, s32[512]{0:T(512)}, u32[]{:S(2)}) copy-start(s32[512]{0:T(512)} %param.10) | copy-start | bytes 6148
  8.5 16.8 %collective-permute-start.9 = (bf16[1024,256]{1,0:T(8,128)(2,1)S(1)}, bf16[1024,256]{1,0:T(8,128)(2,1)S(1)}, u32[]{:S(2)}, u32[]{:S(2)}) collective-permute-start(bf16[1024,256]{1,0:T(8,128)(2,1)S(1)} %pad_maximum_fusion), channel_id=1, source_target_pairs={{0,0},{32,8},{8,32},{40,40},{1,1},{33,9},{9,33},{41,41},{2,2},{34,... | collective-permute-start | bytes 1572872 | tf_op jit(solution)/shard_map/ppermute | solution.py:354
  12.5 9.5 %collective-permute-start.1 = (bf16[512,256]{1,0:T(8,128)(2,1)S(1)}, bf16[512,256]{1,0:T(8,128)(2,1)S(1)}, u32[]{:S(2)}, u32[]{:S(2)}) collective-permute-start(bf16[512,256]{1,0:T(8,128)(2,1)S(1)} %collective-permute-done.refs_1_), channel_id=1, source_target_pairs={{0,1},{1,2},{2,3},{3,4},{4,5},{5,6},{6,7},{7,0},{8,9},{9,10},{10,1... | collective-permute-start | bytes 786440 | tf_op jit(solution)/shard_map/ppermute | solution.py:27
  12.5 9.5 %collective-permute-start.4 = (bf16[512,256]{1,0:T(8,128)(2,1)S(1)}, bf16[512,256]{1,0:T(8,128)(2,1)S(1)}, u32[]{:S(2)}, u32[]{:S(2)}) collective-permute-start(bf16[512,256]{1,0:T(8,128)(2,1)S(1)} %collective-permute-done.3.refs_6_), channel_id=1, source_target_pairs={{0,7},{1,0},{2,1},{3,2},{4,3},{5,4},{6,5},{7,6},{8,15},{9,8},{10,9... | collective-permute-start | bytes 786440 | tf_op jit(solution)/shard_map/ppermute | solution.py:27
  16.4 26.2 %collective-permute-start.7 = (bf16[512,256]{1,0:T(8,128)(2,1)}, bf16[512,256]{1,0:T(8,128)(2,1)}, u32[]{:S(2)}, u32[]{:S(2)}) collective-permute-start(bf16[512,256]{1,0:T(8,128)(2,1)} %constant_dynamic-slice_fusion.2), channel_id=1, source_target_pairs={{0,0},{32,8},{8,32},{40,40},{1,1},{33,9},{9,33},{41,41},{2,2},{34,... | collective-permute-start | bytes 786440 | tf_op jit(solution)/shard_map/ppermute | solution.py:357
  20.0 22.6 %collective-permute-start.8 = (bf16[512,256]{1,0:T(8,128)(2,1)}, bf16[512,256]{1,0:T(8,128)(2,1)}, u32[]{:S(2)}, u32[]{:S(2)}) collective-permute-start(bf16[512,256]{1,0:T(8,128)(2,1)} %constant_dynamic-slice_fusion.2), channel_id=1, source_target_pairs={{8,0},{40,8},{0,32},{32,40},{9,1},{41,9},{1,33},{33,41},{10,2},{42... | collective-permute-start | bytes 786440 | tf_op jit(solution)/shard_map/ppermute | solution.py:357
  22.0 7.6 %collective-permute-start.2 = (bf16[512,256]{1,0:T(8,128)(2,1)S(1)}, bf16[512,256]{1,0:T(8,128)(2,1)S(1)}, u32[]{:S(2)}, u32[]{:S(2)}) collective-permute-start(bf16[512,256]{1,0:T(8,128)(2,1)S(1)} %collective-permute-done.1.refs_2_), channel_id=1, source_target_pairs={{0,1},{1,2},{2,3},{3,4},{4,5},{5,6},{6,7},{7,0},{8,9},{9,10},{10,1... | collective-permute-start | bytes 786440 | tf_op jit(solution)/shard_map/ppermute | solution.py:27
  22.0 7.6 %collective-permute-start.5 = (bf16[512,256]{1,0:T(8,128)(2,1)S(1)}, bf16[512,256]{1,0:T(8,128)(2,1)S(1)}, u32[]{:S(2)}, u32[]{:S(2)}) collective-permute-start(bf16[512,256]{1,0:T(8,128)(2,1)S(1)} %collective-permute-done.4.refs_5_), channel_id=1, source_target_pairs={{0,7},{1,0},{2,1},{3,2},{4,3},{5,4},{6,5},{7,6},{8,15},{9,8},{10,9... | collective-permute-start | bytes 786440 | tf_op jit(solution)/shard_map/ppermute | solution.py:27
  25.3 5.2 %collective-permute-start.10 = (bf16[1024,256]{1,0:T(8,128)(2,1)S(1)}, bf16[1024,256]{1,0:T(8,128)(2,1)S(1)}, u32[]{:S(2)}, u32[]{:S(2)}) collective-permute-start(bf16[1024,256]{1,0:T(8,128)(2,1)S(1)} %collective-permute-done.9.refs_7_.refs_1_), channel_id=1, source_target_pairs={{0,16},{16,0},{1,17},{17,1},{2,18},{18,2},{3,19},{19,3},{4,20},{20... | collective-permute-start | bytes 1572872 | tf_op jit(solution)/shard_map/ppermute | solution.py:375
  30.3 7.9 %collective-permute-start.6 = (bf16[512,256]{1,0:T(8,128)(2,1)}, bf16[512,256]{1,0:T(8,128)(2,1)}, u32[]{:S(2)}, u32[]{:S(2)}) collective-permute-start(bf16[512,256]{1,0:T(8,128)(2,1)} %broadcast_select_fusion.1), channel_id=1, source_target_pairs={{0,1},{1,2},{2,3},{3,4},{4,5},{5,6},{6,7},{7,0},{16,23},{17,16},{1... | collective-permute-start | bytes 786440 | tf_op jit(solution)/shard_map/ppermute | solution.py:38
  39.7 4.9 %copy-start.2 = (f32[512,128]{1,0:T(8,128)}, f32[512,128]{1,0:T(8,128)S(1)}, u32[]{:S(2)}) copy-start(f32[512,128]{1,0:T(8,128)S(1)} %get-tuple-element.28) | copy-start | bytes 786436
  39.8 5.9 %collective-permute-start.15 = (bf16[528,128]{1,0:T(8,128)(2,1)S(1)}, bf16[528,128]{1,0:T(8,128)(2,1)S(1)}, u32[]{:S(2)}, u32[]{:S(2)}) collective-permute-start(bf16[528,128]{1,0:T(8,128)(2,1)S(1)} %get-tuple-element.22), channel_id=1, source_target_pairs={{0,8},{8,0},{1,9},{9,1},{2,10},{10,2},{3,11},{11,3},{4,12},{12,4},... | collective-permute-start | bytes 405512 | tf_op jit(solution)/shard_map/ppermute | solution.py:379
  44.6 12.1 %collective-permute-start.11 = (bf16[512,512]{1,0:T(8,128)(2,1)S(1)}, bf16[512,512]{1,0:T(8,128)(2,1)S(1)}, u32[]{:S(2)}, u32[]{:S(2)}) collective-permute-start(bf16[512,512]{1,0:T(8,128)(2,1)S(1)} %constant_dynamic-update-slice_fusion.refs_8_), channel_id=1, source_target_pairs={{0,64},{64,0},{128,192},{192,128},{1,65},{65,1},{129,193},{193,129... | collective-permute-start | bytes 1572872 | tf_op jit(solution)/shard_map/ppermute | solution.py:396
  45.2 21.7 %collective-permute-start.12 = (bf16[512,512]{1,0:T(8,128)(2,1)S(1)}, bf16[512,512]{1,0:T(8,128)(2,1)}, u32[]{:S(2)}, u32[]{:S(2)}) collective-permute-start(bf16[512,512]{1,0:T(8,128)(2,1)S(1)} %constant_dynamic-update-slice_fusion.refs_8_), channel_id=1, source_target_pairs={{0,16},{16,0},{1,17},{17,1},{2,18},{18,2},{3,19},{19,3},{4,20},{20... | collective-permute-start | bytes 1572872 | tf_op jit(solution)/shard_map/ppermute | solution.py:397
  45.7 0.7 copy-start.3
  56.7 10.1 %collective-permute-start.13 = (bf16[512,512]{1,0:T(8,128)(2,1)S(1)}, bf16[512,512]{1,0:T(8,128)(2,1)}, u32[]{:S(2)}, u32[]{:S(2)}) collective-permute-start(bf16[512,512]{1,0:T(8,128)(2,1)S(1)} %collective-permute-done.11.refs_9_), channel_id=1, source_target_pairs={{0,16},{16,0},{1,17},{17,1},{2,18},{18,2},{3,19},{19,3},{4,20},{20... | collective-permute-start | bytes 1572872 | tf_op jit(solution)/shard_map/ppermute | solution.py:397
  57.8 6.1 %collective-permute-start.17 = (bf16[512,128]{1,0:T(8,128)(2,1)S(1)}, bf16[512,128]{1,0:T(8,128)(2,1)}, u32[]{:S(2)}, u32[]{:S(2)}) collective-permute-start(bf16[512,128]{1,0:T(8,128)(2,1)S(1)} %multiply_convert_fusion.2), channel_id=1, source_target_pairs={{0,1},{1,0},{2,3},{3,2},{4,5},{5,4},{6,7},{7,6},{8,9},{9,8},{10,11... | collective-permute-start | bytes 393224 | tf_op jit(solution)/shard_map/ppermute | solution.py:383
  64.9 10.9 %collective-permute-start.20 = (bf16[528,256]{1,0:T(8,128)(2,1)S(1)}, bf16[528,256]{1,0:T(8,128)(2,1)S(1)}, u32[]{:S(2)}, u32[]{:S(2)}) collective-permute-start(bf16[528,256]{1,0:T(8,128)(2,1)S(1)} %pad_maximum_fusion.2.refs_3_), channel_id=1, source_target_pairs={{0,32},{32,0},{1,33},{33,1},{2,34},{34,2},{3,35},{35,3},{4,36},{36... | collective-permute-start | bytes 811016 | tf_op jit(solution)/shard_map/ppermute | solution.py:387
  69.7 9.9 %collective-permute-start.14 = (bf16[512,256]{1,0:T(8,128)(2,1)S(1)}, bf16[512,256]{1,0:T(8,128)(2,1)S(1)}, u32[]{:S(2)}, u32[]{:S(2)}) collective-permute-start(bf16[512,256]{1,0:T(8,128)(2,1)S(1)} %get-tuple-element.26), channel_id=1, source_target_pairs={{0,8},{8,0},{1,9},{9,1},{2,10},{10,2},{3,11},{11,3},{4,12},{12,4},... | collective-permute-start | bytes 786440 | tf_op jit(solution)/shard_map/ppermute | solution.py:399
  71.6 10.0 %collective-permute-start.18 = (bf16[528,256]{1,0:T(8,128)(2,1)S(1)}, bf16[528,256]{1,0:T(8,128)(2,1)S(1)}, u32[]{:S(2)}, u32[]{:S(2)}) collective-permute-start(bf16[528,256]{1,0:T(8,128)(2,1)S(1)} %pad_maximum_fusion.2.refs_3_), channel_id=1, source_target_pairs={{0,64},{64,128},{128,192},{192,0},{1,65},{65,129},{129,193},{193,1... | collective-permute-start | bytes 811016 | tf_op jit(solution)/shard_map/ppermute | solution.py:27
  73.1 13.4 %collective-permute-start.19 = (bf16[528,256]{1,0:T(8,128)(2,1)S(1)}, bf16[528,256]{1,0:T(8,128)(2,1)S(1)}, u32[]{:S(2)}, u32[]{:S(2)}) collective-permute-start(bf16[528,256]{1,0:T(8,128)(2,1)S(1)} %pad_maximum_fusion.2.refs_3_), channel_id=1, source_target_pairs={{0,192},{64,0},{128,64},{192,128},{1,193},{65,1},{129,65},{193,129... | collective-permute-start | bytes 811016 | tf_op jit(solution)/shard_map/ppermute | solution.py:27
  75.8 10.3 %collective-permute-start.23 = (bf16[528,256]{1,0:T(8,128)(2,1)S(1)}, bf16[528,256]{1,0:T(8,128)(2,1)S(1)}, u32[]{:S(2)}, u32[]{:S(2)}) collective-permute-start(bf16[528,256]{1,0:T(8,128)(2,1)S(1)} %collective-permute-done.20.refs_2_), channel_id=1, source_target_pairs={{0,192},{64,0},{128,64},{192,128},{1,193},{65,1},{129,65},{193,129... | collective-permute-start | bytes 811016 | tf_op jit(solution)/shard_map/ppermute | solution.py:27
  79.7 6.8 %collective-permute-start.16 = (bf16[528,256]{1,0:T(8,128)(2,1)S(1)}, bf16[528,256]{1,0:T(8,128)(2,1)S(1)}, u32[]{:S(2)}, u32[]{:S(2)}) collective-permute-start(bf16[528,256]{1,0:T(8,128)(2,1)S(1)} %pad_maximum_fusion.1.refs_1_), channel_id=1, source_target_pairs={{0,16},{16,0},{1,17},{17,1},{2,18},{18,2},{3,19},{19,3},{4,20},{20... | collective-permute-start | bytes 811016 | tf_op jit(solution)/shard_map/ppermute | solution.py:402
  79.9 14.7 %collective-permute-start.22 = (bf16[528,256]{1,0:T(8,128)(2,1)S(1)}, bf16[528,256]{1,0:T(8,128)(2,1)S(1)}, u32[]{:S(2)}, u32[]{:S(2)}) collective-permute-start(bf16[528,256]{1,0:T(8,128)(2,1)S(1)} %collective-permute-done.20.refs_2_), channel_id=1, source_target_pairs={{0,64},{64,128},{128,192},{192,0},{1,65},{65,129},{129,193},{193,1... | collective-permute-start | bytes 811016 | tf_op jit(solution)/shard_map/ppermute | solution.py:27
  81.5 13.1 %collective-permute-start.21 = (bf16[528,256]{1,0:T(8,128)(2,1)S(1)}, bf16[528,256]{1,0:T(8,128)(2,1)S(1)}, u32[]{:S(2)}, u32[]{:S(2)}) collective-permute-start(bf16[528,256]{1,0:T(8,128)(2,1)S(1)} %collective-permute-done.18.refs_4_), channel_id=1, source_target_pairs={{0,64},{64,128},{128,192},{192,0},{1,65},{65,129},{129,193},{193,1... | collective-permute-start | bytes 811016 | tf_op jit(solution)/shard_map/ppermute | solution.py:27
  86.1 13.4 %collective-permute-start.24 = (bf16[528,256]{1,0:T(8,128)(2,1)S(1)}, bf16[528,256]{1,0:T(8,128)(2,1)S(1)}, u32[]{:S(2)}, u32[]{:S(2)}) collective-permute-start(bf16[528,256]{1,0:T(8,128)(2,1)S(1)} %collective-permute-done.23.refs_5_), channel_id=1, source_target_pairs={{0,192},{64,0},{128,64},{192,128},{1,193},{65,1},{129,65},{193,129... | collective-permute-start | bytes 811016 | tf_op jit(solution)/shard_map/ppermute | solution.py:27
  99.5 7.5 %copy-start.6 = (bf16[1024,256]{1,0:T(8,128)(2,1)S(1)}, bf16[1024,256]{1,0:T(8,128)(2,1)}, u32[]{:S(2)}) copy-start(bf16[1024,256]{1,0:T(8,128)(2,1)} %param.15) | copy-start | bytes 1572868
  101.9 1.6 %collective-permute-start.25 = (bf16[512,256]{1,0:T(8,128)(2,1)S(1)}, bf16[512,256]{1,0:T(8,128)(2,1)S(1)}, u32[]{:S(2)}, u32[]{:S(2)}) collective-permute-start(bf16[512,256]{1,0:T(8,128)(2,1)S(1)} %get-tuple-element.32), channel_id=1, source_target_pairs={{0,16},{16,0},{1,17},{17,1},{2,18},{18,2},{3,19},{19,3},{4,20},{20... | collective-permute-start | bytes 786440 | tf_op jit(solution)/shard_map/ppermute | solution.py:410
  103.7 9.6 %collective-permute-start.26 = (bf16[512,256]{1,0:T(8,128)(2,1)S(1)}, bf16[512,256]{1,0:T(8,128)(2,1)S(1)}, u32[]{:S(2)}, u32[]{:S(2)}) collective-permute-start(bf16[512,256]{1,0:T(8,128)(2,1)S(1)} %multiply_convert_fusion.refs_0_), channel_id=1, source_target_pairs={{0,1},{1,2},{2,3},{3,4},{4,5},{5,6},{6,7},{7,0},{8,9},{9,10},{10,1... | collective-permute-start | bytes 786440 | tf_op jit(solution)/shard_map/ppermute | solution.py:27
  104.3 9.0 %collective-permute-start.29 = (bf16[512,256]{1,0:T(8,128)(2,1)S(1)}, bf16[512,256]{1,0:T(8,128)(2,1)S(1)}, u32[]{:S(2)}, u32[]{:S(2)}) collective-permute-start(bf16[512,256]{1,0:T(8,128)(2,1)S(1)} %multiply_convert_fusion.refs_0_), channel_id=1, source_target_pairs={{0,7},{1,0},{2,1},{3,2},{4,3},{5,4},{6,5},{7,6},{8,15},{9,8},{10,9... | collective-permute-start | bytes 786440 | tf_op jit(solution)/shard_map/ppermute | solution.py:27
  107.0 18.3 %collective-permute-start.33 = (bf16[1024,256]{1,0:T(8,128)(2,1)S(1)}, bf16[1024,256]{1,0:T(8,128)(2,1)S(1)}, u32[]{:S(2)}, u32[]{:S(2)}) collective-permute-start(bf16[1024,256]{1,0:T(8,128)(2,1)S(1)} %copy-done.6), channel_id=1, source_target_pairs={{0,0},{32,8},{8,32},{40,40},{1,1},{33,9},{9,33},{41,41},{2,2},{34,... | collective-permute-start | bytes 1572872 | tf_op jit(solution)/shard_map/ppermute | solution.py:404
  107.7 17.6 %collective-permute-start.35 = (bf16[1024,256]{1,0:T(8,128)(2,1)S(1)}, bf16[1024,256]{1,0:T(8,128)(2,1)S(1)}, u32[]{:S(2)}, u32[]{:S(2)}) collective-permute-start(bf16[1024,256]{1,0:T(8,128)(2,1)S(1)} %copy-done.6), channel_id=1, source_target_pairs={{8,0},{40,8},{0,32},{32,40},{9,1},{41,9},{1,33},{33,41},{10,2},{42... | collective-permute-start | bytes 1572872 | tf_op jit(solution)/shard_map/ppermute | solution.py:404
  113.3 8.7 %collective-permute-start.27 = (bf16[512,256]{1,0:T(8,128)(2,1)S(1)}, bf16[512,256]{1,0:T(8,128)(2,1)S(1)}, u32[]{:S(2)}, u32[]{:S(2)}) collective-permute-start(bf16[512,256]{1,0:T(8,128)(2,1)S(1)} %collective-permute-done.26.refs_1_), channel_id=1, source_target_pairs={{0,1},{1,2},{2,3},{3,4},{4,5},{5,6},{6,7},{7,0},{8,9},{9,10},{10,1... | collective-permute-start | bytes 786440 | tf_op jit(solution)/shard_map/ppermute | solution.py:27
  113.3 8.7 %collective-permute-start.30 = (bf16[512,256]{1,0:T(8,128)(2,1)S(1)}, bf16[512,256]{1,0:T(8,128)(2,1)S(1)}, u32[]{:S(2)}, u32[]{:S(2)}) collective-permute-start(bf16[512,256]{1,0:T(8,128)(2,1)S(1)} %collective-permute-done.29.refs_6_), channel_id=1, source_target_pairs={{0,7},{1,0},{2,1},{3,2},{4,3},{5,4},{6,5},{7,6},{8,15},{9,8},{10,9... | collective-permute-start | bytes 786440 | tf_op jit(solution)/shard_map/ppermute | solution.py:27
  122.0 7.8 %collective-permute-start.28 = (bf16[512,256]{1,0:T(8,128)(2,1)S(1)}, bf16[512,256]{1,0:T(8,128)(2,1)S(1)}, u32[]{:S(2)}, u32[]{:S(2)}) collective-permute-start(bf16[512,256]{1,0:T(8,128)(2,1)S(1)} %collective-permute-done.27.refs_2_), channel_id=1, source_target_pairs={{0,1},{1,2},{2,3},{3,4},{4,5},{5,6},{6,7},{7,0},{8,9},{9,10},{10,1... | collective-permute-start | bytes 786440 | tf_op jit(solution)/shard_map/ppermute | solution.py:27
  122.0 7.8 %collective-permute-start.31 = (bf16[512,256]{1,0:T(8,128)(2,1)S(1)}, bf16[512,256]{1,0:T(8,128)(2,1)S(1)}, u32[]{:S(2)}, u32[]{:S(2)}) collective-permute-start(bf16[512,256]{1,0:T(8,128)(2,1)S(1)} %collective-permute-done.30.refs_5_), channel_id=1, source_target_pairs={{0,7},{1,0},{2,1},{3,2},{4,3},{5,4},{6,5},{7,6},{8,15},{9,8},{10,9... | collective-permute-start | bytes 786440 | tf_op jit(solution)/shard_map/ppermute | solution.py:27
  125.3 4.7 %collective-permute-start.34 = (bf16[1024,256]{1,0:T(8,128)(2,1)S(1)}, bf16[1024,256]{1,0:T(8,128)(2,1)S(1)}, u32[]{:S(2)}, u32[]{:S(2)}) collective-permute-start(bf16[1024,256]{1,0:T(8,128)(2,1)S(1)} %collective-permute-done.33.refs_7_.refs_1_), channel_id=1, source_target_pairs={{0,16},{16,0},{1,17},{17,1},{2,18},{18,2},{3,19},{19,3},{4,20},{20... | collective-permute-start | bytes 1572872 | tf_op jit(solution)/shard_map/ppermute | solution.py:414
  125.3 4.7 %collective-permute-start.36 = (bf16[1024,256]{1,0:T(8,128)(2,1)S(1)}, bf16[1024,256]{1,0:T(8,128)(2,1)S(1)}, u32[]{:S(2)}, u32[]{:S(2)}) collective-permute-start(bf16[1024,256]{1,0:T(8,128)(2,1)S(1)} %collective-permute-done.35.refs_9_.refs_3_), channel_id=1, source_target_pairs={{0,16},{16,0},{1,17},{17,1},{2,18},{18,2},{3,19},{19,3},{4,20},{20... | collective-permute-start | bytes 1572872 | tf_op jit(solution)/shard_map/ppermute | solution.py:414
  129.9 7.7 %collective-permute-start.32 = (bf16[512,256]{1,0:T(8,128)(2,1)S(1)}, bf16[512,256]{1,0:T(8,128)(2,1)S(1)}, u32[]{:S(2)}, u32[]{:S(2)}) collective-permute-start(bf16[512,256]{1,0:T(8,128)(2,1)S(1)} %broadcast_select_fusion), channel_id=1, source_target_pairs={{0,1},{1,2},{2,3},{3,4},{4,5},{5,6},{6,7},{7,0},{16,23},{17,16},{1... | collective-permute-start | bytes 786440 | tf_op jit(solution)/shard_map/ppermute | solution.py:38
  138.5 9.7 %collective-permute-start.37 = (bf16[512,256]{1,0:T(8,128)(2,1)S(1)}, bf16[512,256]{1,0:T(8,128)(2,1)S(1)}, u32[]{:S(2)}, u32[]{:S(2)}) collective-permute-start(bf16[512,256]{1,0:T(8,128)(2,1)S(1)} %get-tuple-element.34), channel_id=1, source_target_pairs={{0,8},{8,0},{1,9},{9,1},{2,10},{10,2},{3,11},{11,3},{4,12},{12,4},... | collective-permute-start | bytes 786440 | tf_op jit(solution)/shard_map/ppermute | solution.py:418

commit v2 on v1

--- a/solution.py
+++ b/solution.py
@@ -209,6 +209,33 @@
     )(scal, *xs, last, *ws)
 
 
+def scale_kernel(keep, got, squares, out, scale):
+    rows = keep.shape[0]
+    below = got[rows:, :].astype(F32)
+    for k in range(rows // HD):
+        at = slice(k * HD, (k + 1) * HD)
+        total = squares[:1, at] + below[k : k + 1] + below[4 + k : 5 + k] + below[8 + k : 9 + k]
+        row = lax.rsqrt(total * (1.0 / D) + norm_eps)
+        column = jnp.broadcast_to(row, (HD, HD)).T
+        out[at, :] = ((keep[at, :] + got[at, :].astype(F32)) * column).astype(BF)
+        scale[at, :] = jnp.concatenate([column, column], axis=1)
+
+
+def scale_rows(keep, got, squares):
+    rows = keep.shape[0]
+    return pl.pallas_call(
+        scale_kernel,
+        out_shape=[
+            jax.ShapeDtypeStruct((rows, HD), BF),
+            jax.ShapeDtypeStruct((rows, 2 * HD), F32),
+        ],
+        in_specs=[VM] * 3,
+        out_specs=[VM] * 2,
+        compiler_params=pltpu.CompilerParams(vmem_limit_bytes=PROJECT_VMEM),
+        name="scale_rows",
+    )(keep, got, squares)
+
+
 PROJECT_VMEM = 10 << 20
 ATTEND_VMEM = 16 << 20
 
@@ -377,9 +404,7 @@
     sums = project_most(scal, xs, kv_w, True)
     kv_keep, kv_send, squares = project_last(scal, 2, last, kv_w, sums)
     kv_got = lax.ppermute(kv_send, "xl", SWAP)
-    sq = squares[0] + kv_got[rows : rows + 12].astype(F32).reshape(3, rows).sum(axis=0)
-    row_scale = lax.rsqrt(sq * (1.0 / D) + norm_eps)[:, None]
-    mine = ((kv_keep + kv_got[:rows].astype(F32)) * row_scale).astype(BF)
+    mine, row_scale = scale_rows(kv_keep, kv_got, squares)
     other = lax.ppermute(mine, "z", [(i, i ^ 1) for i in range(NZ)])
     even = z % 2 == 0
     kv = jnp.concatenate([jnp.where(even, mine, other), jnp.where(even, other, mine)], axis=1)
@@ -403,9 +428,9 @@
 
     ow = [lax.ppermute(out_weight, chip_x, t) for t in (TAKE_0, TAKE_1)]
 
-    part, full = attend(scal, (coef, q, q_other), [kv, kv_up, kv_down], (0, 2, 4))
-    rest = [kv_x, kv_far, kv_x_up, kv_x_down]
-    part = attend(scal, (full,), rest, (1, 6, 3, 5), part)[0]
+    part, full = attend(scal, (coef, q, q_other), [kv, kv_up], (0, 2))
+    rest = [kv_down, kv_x, kv_far, kv_x_up, kv_x_down]
+    part = attend(scal, (full,), rest, (4, 1, 6, 3, 5), part)[0]
     mine, theirs = attend(scal, (full,), [kv_x_far], (7,), part, True)
     back = lax.ppermute(theirs, "core", SWAP)
     attended = ((mine + back.astype(F32)) * inv).astype(BF)

time: 150 us -> 153 us (1.020)
  starting transfers between devices: 52.1 us -> 62.9 us
  waiting for transfers between devices: 61.3 us -> 55.7 us
    ppermute x1, starting transfers between devices: 1.93 us -> 8.17 us  [shards(): kv_x = lax.ppermute(kv, 'xh', SWAP)]
    ppermute x1, waiting for transfers between devices: 10.3 us -> 5.38 us  [shards(): q_w = [qw, lax.ppermute(qw, 'y', [(i, i ^ 1) for i in range(NY)])]]
    ppermute x1, starting transfers between devices: 5.26 us -> 6.96 us  [shards(): o_got = lax.ppermute(o_send, 'xl', SWAP)]
    ppermute x2, starting transfers between devices: 4.95 us -> 6.52 us  [shards(): ow = [lax.ppermute(out_weight, chip_x, t) for t in (TAKE_0, TAKE_1)]]
  transfers between devices with their start and end apart: 38 -> 38, of which waited for: 16 -> 14; matrix products, arithmetic and copies ran while one was open for 7% -> 4% of each run, Pallas kernels for 13% -> 13%
where the time goes in v2:
time: 153 us; the launch traced here: 152 us
  starting transfers between devices  62.9 us (41%)
  waiting for transfers between devices  55.7 us (36%)
  Pallas kernels  23.1 us (15%)
  local copies, waits for them, and re-layouts  5.18 us (3%)
  other arithmetic  4.45 us (3%)
    ppermute x18, starting transfers between devices, shift(): return lax.ppermute(x, axis, [(i, (i + by) % size) for i in range(size)])  28.4 us
    ppermute x18, waiting for transfers between devices, shift(): return lax.ppermute(x, axis, [(i, (i + by) % size) for i in range(size)])  22.3 us
    pallas_call x3, Pallas kernels, attend(): pl.pallas_call(functools.partial(attend_kernel, which, first, final), out...  13.1 us
    ppermute x2, waiting for transfers between devices, ring(): lax.ppermute(last, ('core', 'z'), pairs)  10.9 us
    ppermute x1, starting transfers between devices, shards(): kv_x = lax.ppermute(kv, 'xh', SWAP)  8.17 us
    ppermute x1, starting transfers between devices, shards(): o_got = lax.ppermute(o_send, 'xl', SWAP)  6.96 us
    ppermute x2, starting transfers between devices, shards(): ow = [lax.ppermute(out_weight, chip_x, t) for t in (TAKE_0, TAKE_1)]  6.52 us
    ppermute x1, waiting for transfers between devices, shards(): other = lax.ppermute(mine, 'z', [(i, i ^ 1) for i in range(NZ)])  5.83 us
  transfers between devices with their start and end apart: 38, of which 14 were waited for; matrix products, arithmetic and copies ran while one was open for 4% of the time, Pallas kernels for 13%

profile of v2, /device:TPU:8, one launch (start us, length us, event | category | flops | bytes accessed | tf_op | source)
XLA Modules:
  0.0 151.7 jit_solution(8184928872787013459)
XLA Ops:
  0.0 2.0 %collective-permute-start = (bf16[512,256]{1,0:T(8,128)(2,1)}, bf16[512,256]{1,0:T(8,128)(2,1)S(1)}, u32[]{:S(2)}, u32[]{:S(2)}) collective-permute-start(bf16[512,256]{1,0:T(8,128)(2,1)} %refs_0_.3), channel_id=1, source_target_pairs={{0,1},{1,2},{2,3},{3,4},{4,5},{5,6},{6,7},{7,0},{8,9},{9,10},{10,1... | collective-permute-start | bytes 786440 | tf_op jit(solution)/shard_map/ppermute | solution.py:27
  2.0 4.0 %collective-permute-start.3 = (bf16[512,256]{1,0:T(8,128)(2,1)}, bf16[512,256]{1,0:T(8,128)(2,1)S(1)}, u32[]{:S(2)}, u32[]{:S(2)}) collective-permute-start(bf16[512,256]{1,0:T(8,128)(2,1)} %refs_0_.3), channel_id=1, source_target_pairs={{0,7},{1,0},{2,1},{3,2},{4,3},{5,4},{6,5},{7,6},{8,15},{9,8},{10,9... | collective-permute-start | bytes 786440 | tf_op jit(solution)/shard_map/ppermute | solution.py:27
  6.1 2.3 %constant_dynamic-slice_fusion.1 = (bf16[1024,1,1,128]{3,2,1,0:T(2,128)(2,1)S(1)}, bf16[1024,1,1,128]{3,2,1,0:T(2,128)(2,1)S(1)}) fusion(bf16[1024,8,2,128]{3,2,1,0:T(2,128)(2,1)} %param.13, s32[]{:T(128)S(6)} %select_n.86, s32[]{:T(128)S(6)} %select_n.88, s32[]{:T(128)S(6)} %select_n.89), kind=kLoop, calls=%fused_computation.22 | loop fusion | bytes 1048588 | tf_op jit(solution)/shard_map/dynamic_slice | solution.py:376
  8.4 0.9 pad_maximum_fusion
  9.3 1.7 %collective-permute-start.9 = (bf16[1024,256]{1,0:T(8,128)(2,1)}, bf16[1024,256]{1,0:T(8,128)(2,1)S(1)}, u32[]{:S(2)}, u32[]{:S(2)}) collective-permute-start(bf16[1024,256]{1,0:T(8,128)(2,1)} %pad_maximum_fusion), channel_id=1, source_target_pairs={{0,0},{32,8},{8,32},{40,40},{1,1},{33,9},{9,33},{41,41},{2,2},{34,... | collective-permute-start | bytes 1572872 | tf_op jit(solution)/shard_map/ppermute | solution.py:381
  11.0 1.5 collective-permute-done.refs_1_
  12.5 3.2 %collective-permute-start.4 = (bf16[512,256]{1,0:T(8,128)(2,1)S(1)}, bf16[512,256]{1,0:T(8,128)(2,1)S(1)}, u32[]{:S(2)}, u32[]{:S(2)}) collective-permute-start(bf16[512,256]{1,0:T(8,128)(2,1)S(1)} %collective-permute-done.3.refs_6_), channel_id=1, source_target_pairs={{0,7},{1,0},{2,1},{3,2},{4,3},{5,4},{6,5},{7,6},{8,15},{9,8},{10,9... | collective-permute-start | bytes 786440 | tf_op jit(solution)/shard_map/ppermute | solution.py:27
  15.7 0.7 constant_dynamic-slice_fusion.2
  16.4 3.6 %collective-permute-start.7 = (bf16[512,256]{1,0:T(8,128)(2,1)}, bf16[512,256]{1,0:T(8,128)(2,1)}, u32[]{:S(2)}, u32[]{:S(2)}) collective-permute-start(bf16[512,256]{1,0:T(8,128)(2,1)} %constant_dynamic-slice_fusion.2), channel_id=1, source_target_pairs={{0,0},{32,8},{8,32},{40,40},{1,1},{33,9},{9,33},{41,41},{2,2},{34,... | collective-permute-start | bytes 786440 | tf_op jit(solution)/shard_map/ppermute | solution.py:384
  20.0 2.2 %collective-permute-start.8 = (bf16[512,256]{1,0:T(8,128)(2,1)}, bf16[512,256]{1,0:T(8,128)(2,1)}, u32[]{:S(2)}, u32[]{:S(2)}) collective-permute-start(bf16[512,256]{1,0:T(8,128)(2,1)} %constant_dynamic-slice_fusion.2), channel_id=1, source_target_pairs={{8,0},{40,8},{0,32},{32,40},{9,1},{41,9},{1,33},{33,41},{10,2},{42... | collective-permute-start | bytes 786440 | tf_op jit(solution)/shard_map/ppermute | solution.py:384
  22.3 3.2 %collective-permute-start.5 = (bf16[512,256]{1,0:T(8,128)(2,1)S(1)}, bf16[512,256]{1,0:T(8,128)(2,1)S(1)}, u32[]{:S(2)}, u32[]{:S(2)}) collective-permute-start(bf16[512,256]{1,0:T(8,128)(2,1)S(1)} %collective-permute-done.4.refs_5_), channel_id=1, source_target_pairs={{0,7},{1,0},{2,1},{3,2},{4,3},{5,4},{6,5},{7,6},{8,15},{9,8},{10,9... | collective-permute-start | bytes 786440 | tf_op jit(solution)/shard_map/ppermute | solution.py:27
  25.5 0.1 collective-permute-start.10
  25.7 4.1 %collective-permute-done.2.refs_3_ = bf16[512,256]{1,0:T(8,128)(2,1)S(1)} collective-permute-done((bf16[512,256]{1,0:T(8,128)(2,1)S(1)}, bf16[512,256]{1,0:T(8,128)(2,1)S(1)}, u32[]{:S(2)}, u32[]{:S(2)}) %collective-permute-start.2) | collective-permute-done | bytes 262176 | tf_op jit(solution)/shard_map/ppermute | solution.py:27
  29.9 0.7 broadcast_select_fusion.1
  30.7 0.1 concatenate.18.scal
  30.8 2.3 %project_most.2 = (f32[512,256]{1,0:T(8,128)S(1)}, f32[8,512]{1,0:T(8,128)S(1)}) custom-call(s32[15]{0:T(128)S(1)} %concatenate.18.scal, bf16[512,256]{1,0:T(8,128)(2,1)S(1)} %copy-done.1, bf16[512,256]{1,0:T(8,128)(2,1)S(1)} %collective-permute-done.refs_1_, bf16[512,256]{1,0:T(8,128)(2,1)S(1)} %collective-permute-done.1.refs_2_, ...), custom_call_target="tpu_custom_call" | custom-call | flops 469762048 | bytes 1048576 | tf_op jit(solution)/shard_map/project_most/pallas_call | solution.py:153
  33.1 5.4 %collective-permute-done.6.refs_0_.refs_7_ = bf16[512,256]{1,0:T(8,128)(2,1)} collective-permute-done((bf16[512,256]{1,0:T(8,128)(2,1)}, bf16[512,256]{1,0:T(8,128)(2,1)}, u32[]{:S(2)}, u32[]{:S(2)}) %collective-permute-start.6) | collective-permute-done | bytes 262176 | tf_op jit(solution)/shard_map/ppermute | solution.py:38
  38.5 1.5 %project_last.2 = (f32[512,128]{1,0:T(8,128)S(1)}, bf16[528,128]{1,0:T(8,128)(2,1)S(1)}, f32[8,512]{1,0:T(8,128)S(1)}) custom-call(s32[15]{0:T(128)S(1)} %concatenate.18.scal, bf16[512,256]{1,0:T(8,128)(2,1)} %collective-permute-done.6.refs_0_.refs_7_, bf16[1024,256]{1,0:T(8,128)(2,1)S(1)} %collective-permute-done.9.refs_7_.refs_1_, ...), custom_call_target="tpu_custom_call" | custom-call | tf_op jit(solution)/shard_map/project_last/pallas_call | solution.py:180
  40.0 1.0 constant_dynamic-update-slice_fusion.1
  41.0 1.0 constant_dynamic-update-slice_fusion.refs_8_
  42.0 0.5 collective-permute-start.11
  42.5 3.5 %collective-permute-start.15 = (bf16[528,128]{1,0:T(8,128)(2,1)S(1)}, bf16[528,128]{1,0:T(8,128)(2,1)S(1)}, u32[]{:S(2)}, u32[]{:S(2)}) collective-permute-start(bf16[528,128]{1,0:T(8,128)(2,1)S(1)} %get-tuple-element.24), channel_id=1, source_target_pairs={{0,8},{8,0},{1,9},{9,1},{2,10},{10,2},{3,11},{11,3},{4,12},{12,4},... | collective-permute-start | bytes 405512 | tf_op jit(solution)/shard_map/ppermute | solution.py:406
  46.0 5.4 %collective-permute-done.11.refs_9_ = bf16[512,512]{1,0:T(8,128)(2,1)} collective-permute-done((bf16[512,512]{1,0:T(8,128)(2,1)S(1)}, bf16[512,512]{1,0:T(8,128)(2,1)}, u32[]{:S(2)}, u32[]{:S(2)}) %collective-permute-start.11) | collective-permute-done | bytes 524320 | tf_op jit(solution)/shard_map/ppermute | solution.py:421
  51.4 0.1 scale_rows.1
  51.6 0.2 collective-permute-start.17
  51.9 5.8 %collective-permute-done.17 = bf16[512,128]{1,0:T(8,128)(2,1)} collective-permute-done((bf16[512,128]{1,0:T(8,128)(2,1)S(1)}, bf16[512,128]{1,0:T(8,128)(2,1)}, u32[]{:S(2)}, u32[]{:S(2)}) %collective-permute-start.17) | collective-permute-done | bytes 131104 | tf_op jit(solution)/shard_map/ppermute | solution.py:408
  57.7 0.9 broadcast_select_fusion.3
  58.7 8.2 %collective-permute-start.20 = (bf16[528,256]{1,0:T(8,128)(2,1)S(1)}, bf16[528,256]{1,0:T(8,128)(2,1)S(1)}, u32[]{:S(2)}, u32[]{:S(2)}) collective-permute-start(bf16[528,256]{1,0:T(8,128)(2,1)S(1)} %pad_maximum_fusion.2.refs_3_), channel_id=1, source_target_pairs={{0,32},{32,0},{1,33},{33,1},{2,34},{34,2},{3,35},{35,3},{4,36},{36... | collective-permute-start | bytes 811016 | tf_op jit(solution)/shard_map/ppermute | solution.py:412
  66.8 3.0 %project_all.1 = (f32[512,256]{1,0:T(8,128)S(1)}, bf16[512,256]{1,0:T(8,128)(2,1)S(1)}) custom-call(s32[15]{0:T(128)S(1)} %concatenate.18.scal, bf16[512,256]{1,0:T(8,128)(2,1)S(1)} %copy-done.1, bf16[512,256]{1,0:T(8,128)(2,1)S(1)} %collective-permute-done.refs_1_, bf16[512,256]{1,0:T(8,128)(2,1)S(1)} %collective-permute-done.1.refs_2_, ...), custom_call_target="tpu_custom_call" | custom-call | flops 1073741824 | bytes 2097152 | tf_op jit(solution)/shard_map/project_all/pallas_call | solution.py:198
  69.8 0.1 collective-permute-start.14
  69.9 0.7 multiply_subtract_fusion
  70.6 1.6 %collective-permute-start.18 = (bf16[528,256]{1,0:T(8,128)(2,1)S(1)}, bf16[528,256]{1,0:T(8,128)(2,1)S(1)}, u32[]{:S(2)}, u32[]{:S(2)}) collective-permute-start(bf16[528,256]{1,0:T(8,128)(2,1)S(1)} %pad_maximum_fusion.2.refs_3_), channel_id=1, source_target_pairs={{0,64},{64,128},{128,192},{192,0},{1,65},{65,129},{129,193},{193,1... | collective-permute-start | bytes 811016 | tf_op jit(solution)/shard_map/ppermute | solution.py:27
  72.2 1.6 %collective-permute-done.20.refs_3_ = bf16[528,256]{1,0:T(8,128)(2,1)S(1)} collective-permute-done((bf16[528,256]{1,0:T(8,128)(2,1)S(1)}, bf16[528,256]{1,0:T(8,128)(2,1)S(1)}, u32[]{:S(2)}, u32[]{:S(2)}) %collective-permute-start.20) | collective-permute-done | bytes 270368 | tf_op jit(solution)/shard_map/ppermute | solution.py:412
  73.8 0.4 collective-permute-start.23
  74.2 3.8 %collective-permute-done.14 = bf16[512,256]{1,0:T(8,128)(2,1)S(1)} collective-permute-done((bf16[512,256]{1,0:T(8,128)(2,1)S(1)}, bf16[512,256]{1,0:T(8,128)(2,1)S(1)}, u32[]{:S(2)}, u32[]{:S(2)}) %collective-permute-start.14) | collective-permute-done | bytes 262176 | tf_op jit(solution)/shard_map/ppermute | solution.py:424
  78.0 0.1 multiply_convert_fusion.1
  78.1 0.1 collective-permute-start.16
  78.2 0.5 collective-permute-start.19
  78.8 1.6 %collective-permute-start.22 = (bf16[528,256]{1,0:T(8,128)(2,1)S(1)}, bf16[528,256]{1,0:T(8,128)(2,1)S(1)}, u32[]{:S(2)}, u32[]{:S(2)}) collective-permute-start(bf16[528,256]{1,0:T(8,128)(2,1)S(1)} %collective-permute-done.20.refs_3_), channel_id=1, source_target_pairs={{0,64},{64,128},{128,192},{192,0},{1,65},{65,129},{129,193},{193,1... | collective-permute-start | bytes 811016 | tf_op jit(solution)/shard_map/ppermute | solution.py:27
  80.4 1.6 %collective-permute-start.21 = (bf16[528,256]{1,0:T(8,128)(2,1)S(1)}, bf16[528,256]{1,0:T(8,128)(2,1)S(1)}, u32[]{:S(2)}, u32[]{:S(2)}) collective-permute-start(bf16[528,256]{1,0:T(8,128)(2,1)S(1)} %collective-permute-done.18.refs_4_), channel_id=1, source_target_pairs={{0,64},{64,128},{128,192},{192,0},{1,65},{65,129},{129,193},{193,1... | collective-permute-start | bytes 811016 | tf_op jit(solution)/shard_map/ppermute | solution.py:27
  82.0 0.5 collective-permute-start.24
  82.5 4.5 %attend.3 = (f32[2,512,256]{2,1,0:T(8,128)S(1)}, bf16[2,2,512,256]{3,2,1,0:T(8,128)(2,1)S(1)}) custom-call(s32[15]{0:T(128)S(1)} %concatenate.18.scal, f32[2,128]{1,0:T(2,128)S(1)} %select_select_fusion.refs_0_, bf16[528,256]{1,0:T(8,128)(2,1)S(1)} %pad_maximum_fusion.1.refs_1_, bf16[528,256]{1,0:T(8,128)(2,1)S(1)} %collective-permute-done.16.refs_2_, ...), custom_call_target="tpu_custom_call" | custom-call | flops 2147483648 | bytes 1048576 | tf_op jit(solution)/shard_map/attend/pallas_call | solution.py:354
  87.0 0.7 collective-permute-done.19.refs_2_
  87.7 6.7 %collective-permute-done.21.refs_4_ = bf16[528,256]{1,0:T(8,128)(2,1)S(1)} collective-permute-done((bf16[528,256]{1,0:T(8,128)(2,1)S(1)}, bf16[528,256]{1,0:T(8,128)(2,1)S(1)}, u32[]{:S(2)}, u32[]{:S(2)}) %collective-permute-start.21) | collective-permute-done | bytes 270368 | tf_op jit(solution)/shard_map/ppermute | solution.py:27
  94.4 6.3 %attend.4.refs_1_ = f32[2,512,256]{2,1,0:T(8,128)S(1)} custom-call(s32[15]{0:T(128)S(1)} %concatenate.18.scal, bf16[2,2,512,256]{3,2,1,0:T(8,128)(2,1)S(1)} %get-tuple-element.33.refs_0_, f32[2,512,256]{2,1,0:T(8,128)S(1)} %get-tuple-element.34.refs_1_, bf16[528,256]{1,0:T(8,128)(2,1)S(1)} %collective-permute-done.19.refs_2_, ...), custom_call_target="tpu_custom_call" | custom-call | flops 5368709120 | bytes 1048576 | tf_op jit(solution)/shard_map/attend/pallas_call | solution.py:354
  100.7 2.4 %attend.5 = (f32[512,256]{1,0:T(8,128)S(1)}, bf16[512,256]{1,0:T(8,128)(2,1)S(1)}) custom-call(s32[15]{0:T(128)S(1)} %concatenate.18.scal, bf16[2,2,512,256]{3,2,1,0:T(8,128)(2,1)S(1)} %get-tuple-element.33.refs_0_, f32[2,512,256]{2,1,0:T(8,128)S(1)} %attend.4.refs_1_, bf16[528,256]{1,0:T(8,128)(2,1)S(1)} %collective-permute-done.24.refs_2_), custom_call_target="tpu_custom_call" | custom-call | flops 1073741824 | bytes 1048576 | tf_op jit(solution)/shard_map/attend/pallas_call | solution.py:354
  103.0 0.1 collective-permute-start.25
  103.2 1.5 collective-permute-done.25
  104.7 0.1 multiply_convert_fusion.refs_0_
  104.8 0.6 collective-permute-start.26
  105.5 2.7 %collective-permute-start.29 = (bf16[512,256]{1,0:T(8,128)(2,1)S(1)}, bf16[512,256]{1,0:T(8,128)(2,1)S(1)}, u32[]{:S(2)}, u32[]{:S(2)}) collective-permute-start(bf16[512,256]{1,0:T(8,128)(2,1)S(1)} %multiply_convert_fusion.refs_0_), channel_id=1, source_target_pairs={{0,7},{1,0},{2,1},{3,2},{4,3},{5,4},{6,5},{7,6},{8,15},{9,8},{10,9... | collective-permute-start | bytes 786440 | tf_op jit(solution)/shard_map/ppermute | solution.py:27
  108.1 0.7 collective-permute-start.33
  108.8 5.8 %collective-permute-start.35 = (bf16[1024,256]{1,0:T(8,128)(2,1)S(1)}, bf16[1024,256]{1,0:T(8,128)(2,1)S(1)}, u32[]{:S(2)}, u32[]{:S(2)}) collective-permute-start(bf16[1024,256]{1,0:T(8,128)(2,1)S(1)} %copy-done.4), channel_id=1, source_target_pairs={{8,0},{40,8},{0,32},{32,40},{9,1},{41,9},{1,33},{33,41},{10,2},{42... | collective-permute-start | bytes 1572872 | tf_op jit(solution)/shard_map/ppermute | solution.py:429
  114.7 3.2 %collective-permute-start.30 = (bf16[512,256]{1,0:T(8,128)(2,1)S(1)}, bf16[512,256]{1,0:T(8,128)(2,1)S(1)}, u32[]{:S(2)}, u32[]{:S(2)}) collective-permute-start(bf16[512,256]{1,0:T(8,128)(2,1)S(1)} %collective-permute-done.29.refs_6_), channel_id=1, source_target_pairs={{0,7},{1,0},{2,1},{3,2},{4,3},{5,4},{6,5},{7,6},{8,15},{9,8},{10,9... | collective-permute-start | bytes 786440 | tf_op jit(solution)/shard_map/ppermute | solution.py:27
  117.9 5.3 %collective-permute-done.27.refs_2_ = bf16[512,256]{1,0:T(8,128)(2,1)S(1)} collective-permute-done((bf16[512,256]{1,0:T(8,128)(2,1)S(1)}, bf16[512,256]{1,0:T(8,128)(2,1)S(1)}, u32[]{:S(2)}, u32[]{:S(2)}) %collective-permute-start.27) | collective-permute-done | bytes 262176 | tf_op jit(solution)/shard_map/ppermute | solution.py:27
  123.2 3.2 %collective-permute-start.31 = (bf16[512,256]{1,0:T(8,128)(2,1)S(1)}, bf16[512,256]{1,0:T(8,128)(2,1)S(1)}, u32[]{:S(2)}, u32[]{:S(2)}) collective-permute-start(bf16[512,256]{1,0:T(8,128)(2,1)S(1)} %collective-permute-done.30.refs_5_), channel_id=1, source_target_pairs={{0,7},{1,0},{2,1},{3,2},{4,3},{5,4},{6,5},{7,6},{8,15},{9,8},{10,9... | collective-permute-start | bytes 786440 | tf_op jit(solution)/shard_map/ppermute | solution.py:27
  126.5 0.5 collective-permute-start.36
  127.0 3.9 %collective-permute-done.28.refs_3_ = bf16[512,256]{1,0:T(8,128)(2,1)S(1)} collective-permute-done((bf16[512,256]{1,0:T(8,128)(2,1)S(1)}, bf16[512,256]{1,0:T(8,128)(2,1)S(1)}, u32[]{:S(2)}, u32[]{:S(2)}) %collective-permute-start.28) | collective-permute-done | bytes 262176 | tf_op jit(solution)/shard_map/ppermute | solution.py:27
  131.0 2.0 %project_most.3.refs_5_ = f32[512,512]{1,0:T(8,128)S(1)} custom-call(s32[15]{0:T(128)S(1)} %concatenate.18.scal, bf16[512,256]{1,0:T(8,128)(2,1)S(1)} %multiply_convert_fusion.refs_0_, bf16[512,256]{1,0:T(8,128)(2,1)S(1)} %collective-permute-done.26.refs_1_, bf16[512,256]{1,0:T(8,128)(2,1)S(1)} %collective-permute-done.27.refs_2_, ...), custom_call_target="tpu_custom_call" | custom-call | flops 939524096 | bytes 2097152 | tf_op jit(solution)/shard_map/project_most/pallas_call | solution.py:153
  133.1 5.5 %collective-permute-done.32.refs_0_ = bf16[512,256]{1,0:T(8,128)(2,1)S(1)} collective-permute-done((bf16[512,256]{1,0:T(8,128)(2,1)S(1)}, bf16[512,256]{1,0:T(8,128)(2,1)S(1)}, u32[]{:S(2)}, u32[]{:S(2)}) %collective-permute-start.32) | collective-permute-done | bytes 262176 | tf_op jit(solution)/shard_map/ppermute | solution.py:38
  138.6 0.9 project_last.3
  139.5 7.0 %collective-permute-start.37 = (bf16[512,256]{1,0:T(8,128)(2,1)S(1)}, bf16[512,256]{1,0:T(8,128)(2,1)S(1)}, u32[]{:S(2)}, u32[]{:S(2)}) collective-permute-start(bf16[512,256]{1,0:T(8,128)(2,1)S(1)} %get-tuple-element.38), channel_id=1, source_target_pairs={{0,8},{8,0},{1,9},{9,1},{2,10},{10,2},{3,11},{11,3},{4,12},{12,4},... | collective-permute-start | bytes 786440 | tf_op jit(solution)/shard_map/ppermute | solution.py:443
  146.5 4.4 %collective-permute-done.37 = bf16[512,256]{1,0:T(8,128)(2,1)S(1)} collective-permute-done((bf16[512,256]{1,0:T(8,128)(2,1)S(1)}, bf16[512,256]{1,0:T(8,128)(2,1)S(1)}, u32[]{:S(2)}, u32[]{:S(2)}) %collective-permute-start.37) | collective-permute-done | bytes 262176 | tf_op jit(solution)/shard_map/ppermute | solution.py:443
  150.9 0.8 add_convert_fusion
  (60 shorter events, 0.6 us)
Async XLA Ops:
  0.0 15.7 %copy-start = (bf16[1024,256]{1,0:T(8,128)(2,1)S(1)}, bf16[1024,256]{1,0:T(8,128)(2,1)}, u32[]{:S(2)}) copy-start(bf16[1024,256]{1,0:T(8,128)(2,1)} %param.12) | copy-start | bytes 1572868
  0.0 25.5 %copy-start.6 = (s32[8]{0:T(128)S(1)}, s32[8]{0:T(128)}, u32[]{:S(2)}) copy-start(s32[8]{0:T(128)} %constant.108) | copy-start | bytes 100
  0.0 30.6 %copy-start.3 = (s32[8]{0:T(128)S(1)}, s32[8]{0:T(128)}, u32[]{:S(2)}) copy-start(s32[8]{0:T(128)} %constant.104.clone) | copy-start | bytes 100
  0.0 30.8 %copy-start.1 = (bf16[512,256]{1,0:T(8,128)(2,1)S(1)}, bf16[512,256]{1,0:T(8,128)(2,1)}, u32[]{:S(2)}) copy-start(bf16[512,256]{1,0:T(8,128)(2,1)} %refs_0_.3) | copy-start | bytes 786436
  0.0 25.6 %copy-start.5 = (s32[4]{0:T(128)S(1)}, s32[4]{0:T(128)}, u32[]{:S(2)}) copy-start(s32[4]{0:T(128)} %param.11) | copy-start | bytes 52
  0.0 12.4 %collective-permute-start = (bf16[512,256]{1,0:T(8,128)(2,1)}, bf16[512,256]{1,0:T(8,128)(2,1)S(1)}, u32[]{:S(2)}, u32[]{:S(2)}) collective-permute-start(bf16[512,256]{1,0:T(8,128)(2,1)} %refs_0_.3), channel_id=1, source_target_pairs={{0,1},{1,2},{2,3},{3,4},{4,5},{5,6},{6,7},{7,0},{8,9},{9,10},{10,1... | collective-permute-start | bytes 786440 | tf_op jit(solution)/shard_map/ppermute | solution.py:27
  2.0 10.5 %collective-permute-start.3 = (bf16[512,256]{1,0:T(8,128)(2,1)}, bf16[512,256]{1,0:T(8,128)(2,1)S(1)}, u32[]{:S(2)}, u32[]{:S(2)}) collective-permute-start(bf16[512,256]{1,0:T(8,128)(2,1)} %refs_0_.3), channel_id=1, source_target_pairs={{0,7},{1,0},{2,1},{3,2},{4,3},{5,4},{6,5},{7,6},{8,15},{9,8},{10,9... | collective-permute-start | bytes 786440 | tf_op jit(solution)/shard_map/ppermute | solution.py:27
  8.4 43.4 %copy-start.2 = (s32[512]{0:T(512)S(1)}, s32[512]{0:T(512)}, u32[]{:S(2)}) copy-start(s32[512]{0:T(512)} %param.10) | copy-start | bytes 6148
  9.3 16.2 %collective-permute-start.9 = (bf16[1024,256]{1,0:T(8,128)(2,1)}, bf16[1024,256]{1,0:T(8,128)(2,1)S(1)}, u32[]{:S(2)}, u32[]{:S(2)}) collective-permute-start(bf16[1024,256]{1,0:T(8,128)(2,1)} %pad_maximum_fusion), channel_id=1, source_target_pairs={{0,0},{32,8},{8,32},{40,40},{1,1},{33,9},{9,33},{41,41},{2,2},{34,... | collective-permute-start | bytes 1572872 | tf_op jit(solution)/shard_map/ppermute | solution.py:381
  12.5 9.8 %collective-permute-start.1 = (bf16[512,256]{1,0:T(8,128)(2,1)S(1)}, bf16[512,256]{1,0:T(8,128)(2,1)S(1)}, u32[]{:S(2)}, u32[]{:S(2)}) collective-permute-start(bf16[512,256]{1,0:T(8,128)(2,1)S(1)} %collective-permute-done.refs_1_), channel_id=1, source_target_pairs={{0,1},{1,2},{2,3},{3,4},{4,5},{5,6},{6,7},{7,0},{8,9},{9,10},{10,1... | collective-permute-start | bytes 786440 | tf_op jit(solution)/shard_map/ppermute | solution.py:27
  12.5 9.8 %collective-permute-start.4 = (bf16[512,256]{1,0:T(8,128)(2,1)S(1)}, bf16[512,256]{1,0:T(8,128)(2,1)S(1)}, u32[]{:S(2)}, u32[]{:S(2)}) collective-permute-start(bf16[512,256]{1,0:T(8,128)(2,1)S(1)} %collective-permute-done.3.refs_6_), channel_id=1, source_target_pairs={{0,7},{1,0},{2,1},{3,2},{4,3},{5,4},{6,5},{7,6},{8,15},{9,8},{10,9... | collective-permute-start | bytes 786440 | tf_op jit(solution)/shard_map/ppermute | solution.py:27
  16.4 23.6 %collective-permute-start.7 = (bf16[512,256]{1,0:T(8,128)(2,1)}, bf16[512,256]{1,0:T(8,128)(2,1)}, u32[]{:S(2)}, u32[]{:S(2)}) collective-permute-start(bf16[512,256]{1,0:T(8,128)(2,1)} %constant_dynamic-slice_fusion.2), channel_id=1, source_target_pairs={{0,0},{32,8},{8,32},{40,40},{1,1},{33,9},{9,33},{41,41},{2,2},{34,... | collective-permute-start | bytes 786440 | tf_op jit(solution)/shard_map/ppermute | solution.py:384
  20.0 20.0 %collective-permute-start.8 = (bf16[512,256]{1,0:T(8,128)(2,1)}, bf16[512,256]{1,0:T(8,128)(2,1)}, u32[]{:S(2)}, u32[]{:S(2)}) collective-permute-start(bf16[512,256]{1,0:T(8,128)(2,1)} %constant_dynamic-slice_fusion.2), channel_id=1, source_target_pairs={{8,0},{40,8},{0,32},{32,40},{9,1},{41,9},{1,33},{33,41},{10,2},{42... | collective-permute-start | bytes 786440 | tf_op jit(solution)/shard_map/ppermute | solution.py:384
  22.3 7.6 %collective-permute-start.2 = (bf16[512,256]{1,0:T(8,128)(2,1)S(1)}, bf16[512,256]{1,0:T(8,128)(2,1)S(1)}, u32[]{:S(2)}, u32[]{:S(2)}) collective-permute-start(bf16[512,256]{1,0:T(8,128)(2,1)S(1)} %collective-permute-done.1.refs_2_), channel_id=1, source_target_pairs={{0,1},{1,2},{2,3},{3,4},{4,5},{5,6},{6,7},{7,0},{8,9},{9,10},{10,1... | collective-permute-start | bytes 786440 | tf_op jit(solution)/shard_map/ppermute | solution.py:27
  22.3 7.6 %collective-permute-start.5 = (bf16[512,256]{1,0:T(8,128)(2,1)S(1)}, bf16[512,256]{1,0:T(8,128)(2,1)S(1)}, u32[]{:S(2)}, u32[]{:S(2)}) collective-permute-start(bf16[512,256]{1,0:T(8,128)(2,1)S(1)} %collective-permute-done.4.refs_5_), channel_id=1, source_target_pairs={{0,7},{1,0},{2,1},{3,2},{4,3},{5,4},{6,5},{7,6},{8,15},{9,8},{10,9... | collective-permute-start | bytes 786440 | tf_op jit(solution)/shard_map/ppermute | solution.py:27
  25.5 5.2 %collective-permute-start.10 = (bf16[1024,256]{1,0:T(8,128)(2,1)S(1)}, bf16[1024,256]{1,0:T(8,128)(2,1)S(1)}, u32[]{:S(2)}, u32[]{:S(2)}) collective-permute-start(bf16[1024,256]{1,0:T(8,128)(2,1)S(1)} %collective-permute-done.9.refs_7_.refs_1_), channel_id=1, source_target_pairs={{0,16},{16,0},{1,17},{17,1},{2,18},{18,2},{3,19},{19,3},{4,20},{20... | collective-permute-start | bytes 1572872 | tf_op jit(solution)/shard_map/ppermute | solution.py:402
  30.6 7.9 %collective-permute-start.6 = (bf16[512,256]{1,0:T(8,128)(2,1)}, bf16[512,256]{1,0:T(8,128)(2,1)}, u32[]{:S(2)}, u32[]{:S(2)}) collective-permute-start(bf16[512,256]{1,0:T(8,128)(2,1)} %broadcast_select_fusion.1), channel_id=1, source_target_pairs={{0,1},{1,2},{2,3},{3,4},{4,5},{5,6},{6,7},{7,0},{16,23},{17,16},{1... | collective-permute-start | bytes 786440 | tf_op jit(solution)/shard_map/ppermute | solution.py:38
  42.0 9.4 %collective-permute-start.11 = (bf16[512,512]{1,0:T(8,128)(2,1)S(1)}, bf16[512,512]{1,0:T(8,128)(2,1)}, u32[]{:S(2)}, u32[]{:S(2)}) collective-permute-start(bf16[512,512]{1,0:T(8,128)(2,1)S(1)} %constant_dynamic-update-slice_fusion.refs_8_), channel_id=1, source_target_pairs={{0,64},{64,0},{128,192},{192,128},{1,65},{65,1},{129,193},{193,129... | collective-permute-start | bytes 1572872 | tf_op jit(solution)/shard_map/ppermute | solution.py:421
  42.5 8.9 %collective-permute-start.15 = (bf16[528,128]{1,0:T(8,128)(2,1)S(1)}, bf16[528,128]{1,0:T(8,128)(2,1)S(1)}, u32[]{:S(2)}, u32[]{:S(2)}) collective-permute-start(bf16[528,128]{1,0:T(8,128)(2,1)S(1)} %get-tuple-element.24), channel_id=1, source_target_pairs={{0,8},{8,0},{1,9},{9,1},{2,10},{10,2},{3,11},{11,3},{4,12},{12,4},... | collective-permute-start | bytes 405512 | tf_op jit(solution)/shard_map/ppermute | solution.py:406
  46.0 20.8 %collective-permute-start.12 = (bf16[512,512]{1,0:T(8,128)(2,1)S(1)}, bf16[512,512]{1,0:T(8,128)(2,1)}, u32[]{:S(2)}, u32[]{:S(2)}) collective-permute-start(bf16[512,512]{1,0:T(8,128)(2,1)S(1)} %constant_dynamic-update-slice_fusion.refs_8_), channel_id=1, source_target_pairs={{0,16},{16,0},{1,17},{17,1},{2,18},{18,2},{3,19},{19,3},{4,20},{20... | collective-permute-start | bytes 1572872 | tf_op jit(solution)/shard_map/ppermute | solution.py:422
  51.4 15.4 %collective-permute-start.13 = (bf16[512,512]{1,0:T(8,128)(2,1)}, bf16[512,512]{1,0:T(8,128)(2,1)}, u32[]{:S(2)}, u32[]{:S(2)}) collective-permute-start(bf16[512,512]{1,0:T(8,128)(2,1)} %collective-permute-done.11.refs_9_), channel_id=1, source_target_pairs={{0,16},{16,0},{1,17},{17,1},{2,18},{18,2},{3,19},{19,3},{4,20},{20... | collective-permute-start | bytes 1572872 | tf_op jit(solution)/shard_map/ppermute | solution.py:422
  51.6 6.1 %collective-permute-start.17 = (bf16[512,128]{1,0:T(8,128)(2,1)S(1)}, bf16[512,128]{1,0:T(8,128)(2,1)}, u32[]{:S(2)}, u32[]{:S(2)}) collective-permute-start(bf16[512,128]{1,0:T(8,128)(2,1)S(1)} %get-tuple-element.32), channel_id=1, source_target_pairs={{0,1},{1,0},{2,3},{3,2},{4,5},{5,4},{6,7},{7,6},{8,9},{9,8},{10,11... | collective-permute-start | bytes 393224 | tf_op jit(solution)/shard_map/ppermute | solution.py:408
  58.7 15.1 %collective-permute-start.20 = (bf16[528,256]{1,0:T(8,128)(2,1)S(1)}, bf16[528,256]{1,0:T(8,128)(2,1)S(1)}, u32[]{:S(2)}, u32[]{:S(2)}) collective-permute-start(bf16[528,256]{1,0:T(8,128)(2,1)S(1)} %pad_maximum_fusion.2.refs_3_), channel_id=1, source_target_pairs={{0,32},{32,0},{1,33},{33,1},{2,34},{34,2},{3,35},{35,3},{4,36},{36... | collective-permute-start | bytes 811016 | tf_op jit(solution)/shard_map/ppermute | solution.py:412
  69.8 8.2 %collective-permute-start.14 = (bf16[512,256]{1,0:T(8,128)(2,1)S(1)}, bf16[512,256]{1,0:T(8,128)(2,1)S(1)}, u32[]{:S(2)}, u32[]{:S(2)}) collective-permute-start(bf16[512,256]{1,0:T(8,128)(2,1)S(1)} %get-tuple-element.28), channel_id=1, source_target_pairs={{0,8},{8,0},{1,9},{9,1},{2,10},{10,2},{3,11},{11,3},{4,12},{12,4},... | collective-permute-start | bytes 786440 | tf_op jit(solution)/shard_map/ppermute | solution.py:424
  70.6 9.7 %collective-permute-start.18 = (bf16[528,256]{1,0:T(8,128)(2,1)S(1)}, bf16[528,256]{1,0:T(8,128)(2,1)S(1)}, u32[]{:S(2)}, u32[]{:S(2)}) collective-permute-start(bf16[528,256]{1,0:T(8,128)(2,1)S(1)} %pad_maximum_fusion.2.refs_3_), channel_id=1, source_target_pairs={{0,64},{64,128},{128,192},{192,0},{1,65},{65,129},{129,193},{193,1... | collective-permute-start | bytes 811016 | tf_op jit(solution)/shard_map/ppermute | solution.py:27
  73.8 8.2 %collective-permute-start.23 = (bf16[528,256]{1,0:T(8,128)(2,1)S(1)}, bf16[528,256]{1,0:T(8,128)(2,1)S(1)}, u32[]{:S(2)}, u32[]{:S(2)}) collective-permute-start(bf16[528,256]{1,0:T(8,128)(2,1)S(1)} %collective-permute-done.20.refs_3_), channel_id=1, source_target_pairs={{0,192},{64,0},{128,64},{192,128},{1,193},{65,1},{129,65},{193,129... | collective-permute-start | bytes 811016 | tf_op jit(solution)/shard_map/ppermute | solution.py:27
  78.1 4.3 %collective-permute-start.16 = (bf16[528,256]{1,0:T(8,128)(2,1)S(1)}, bf16[528,256]{1,0:T(8,128)(2,1)S(1)}, u32[]{:S(2)}, u32[]{:S(2)}) collective-permute-start(bf16[528,256]{1,0:T(8,128)(2,1)S(1)} %pad_maximum_fusion.1.refs_1_), channel_id=1, source_target_pairs={{0,16},{16,0},{1,17},{17,1},{2,18},{18,2},{3,19},{19,3},{4,20},{20... | collective-permute-start | bytes 811016 | tf_op jit(solution)/shard_map/ppermute | solution.py:427
  78.2 9.4 %collective-permute-start.19 = (bf16[528,256]{1,0:T(8,128)(2,1)S(1)}, bf16[528,256]{1,0:T(8,128)(2,1)S(1)}, u32[]{:S(2)}, u32[]{:S(2)}) collective-permute-start(bf16[528,256]{1,0:T(8,128)(2,1)S(1)} %pad_maximum_fusion.2.refs_3_), channel_id=1, source_target_pairs={{0,192},{64,0},{128,64},{192,128},{1,193},{65,1},{129,65},{193,129... | collective-permute-start | bytes 811016 | tf_op jit(solution)/shard_map/ppermute | solution.py:27
  78.8 15.6 %collective-permute-start.22 = (bf16[528,256]{1,0:T(8,128)(2,1)S(1)}, bf16[528,256]{1,0:T(8,128)(2,1)S(1)}, u32[]{:S(2)}, u32[]{:S(2)}) collective-permute-start(bf16[528,256]{1,0:T(8,128)(2,1)S(1)} %collective-permute-done.20.refs_3_), channel_id=1, source_target_pairs={{0,64},{64,128},{128,192},{192,0},{1,65},{65,129},{129,193},{193,1... | collective-permute-start | bytes 811016 | tf_op jit(solution)/shard_map/ppermute | solution.py:27
  80.4 14.0 %collective-permute-start.21 = (bf16[528,256]{1,0:T(8,128)(2,1)S(1)}, bf16[528,256]{1,0:T(8,128)(2,1)S(1)}, u32[]{:S(2)}, u32[]{:S(2)}) collective-permute-start(bf16[528,256]{1,0:T(8,128)(2,1)S(1)} %collective-permute-done.18.refs_4_), channel_id=1, source_target_pairs={{0,64},{64,128},{128,192},{192,0},{1,65},{65,129},{129,193},{193,1... | collective-permute-start | bytes 811016 | tf_op jit(solution)/shard_map/ppermute | solution.py:27
  82.0 18.7 %collective-permute-start.24 = (bf16[528,256]{1,0:T(8,128)(2,1)S(1)}, bf16[528,256]{1,0:T(8,128)(2,1)S(1)}, u32[]{:S(2)}, u32[]{:S(2)}) collective-permute-start(bf16[528,256]{1,0:T(8,128)(2,1)S(1)} %collective-permute-done.23.refs_6_), channel_id=1, source_target_pairs={{0,192},{64,0},{128,64},{192,128},{1,193},{65,1},{129,65},{193,129... | collective-permute-start | bytes 811016 | tf_op jit(solution)/shard_map/ppermute | solution.py:27
  100.7 7.5 %copy-start.4 = (bf16[1024,256]{1,0:T(8,128)(2,1)S(1)}, bf16[1024,256]{1,0:T(8,128)(2,1)}, u32[]{:S(2)}) copy-start(bf16[1024,256]{1,0:T(8,128)(2,1)} %param.15) | copy-start | bytes 1572868
  103.0 1.6 %collective-permute-start.25 = (bf16[512,256]{1,0:T(8,128)(2,1)S(1)}, bf16[512,256]{1,0:T(8,128)(2,1)S(1)}, u32[]{:S(2)}, u32[]{:S(2)}) collective-permute-start(bf16[512,256]{1,0:T(8,128)(2,1)S(1)} %get-tuple-element.36), channel_id=1, source_target_pairs={{0,16},{16,0},{1,17},{17,1},{2,18},{18,2},{3,19},{19,3},{4,20},{20... | collective-permute-start | bytes 786440 | tf_op jit(solution)/shard_map/ppermute | solution.py:435
  104.8 9.9 %collective-permute-start.26 = (bf16[512,256]{1,0:T(8,128)(2,1)S(1)}, bf16[512,256]{1,0:T(8,128)(2,1)S(1)}, u32[]{:S(2)}, u32[]{:S(2)}) collective-permute-start(bf16[512,256]{1,0:T(8,128)(2,1)S(1)} %multiply_convert_fusion.refs_0_), channel_id=1, source_target_pairs={{0,1},{1,2},{2,3},{3,4},{4,5},{5,6},{6,7},{7,0},{8,9},{9,10},{10,1... | collective-permute-start | bytes 786440 | tf_op jit(solution)/shard_map/ppermute | solution.py:27
  105.5 9.2 %collective-permute-start.29 = (bf16[512,256]{1,0:T(8,128)(2,1)S(1)}, bf16[512,256]{1,0:T(8,128)(2,1)S(1)}, u32[]{:S(2)}, u32[]{:S(2)}) collective-permute-start(bf16[512,256]{1,0:T(8,128)(2,1)S(1)} %multiply_convert_fusion.refs_0_), channel_id=1, source_target_pairs={{0,7},{1,0},{2,1},{3,2},{4,3},{5,4},{6,5},{7,6},{8,15},{9,8},{10,9... | collective-permute-start | bytes 786440 | tf_op jit(solution)/shard_map/ppermute | solution.py:27
  108.1 18.3 %collective-permute-start.33 = (bf16[1024,256]{1,0:T(8,128)(2,1)S(1)}, bf16[1024,256]{1,0:T(8,128)(2,1)S(1)}, u32[]{:S(2)}, u32[]{:S(2)}) collective-permute-start(bf16[1024,256]{1,0:T(8,128)(2,1)S(1)} %copy-done.4), channel_id=1, source_target_pairs={{0,0},{32,8},{8,32},{40,40},{1,1},{33,9},{9,33},{41,41},{2,2},{34,... | collective-permute-start | bytes 1572872 | tf_op jit(solution)/shard_map/ppermute | solution.py:429
  108.8 17.6 %collective-permute-start.35 = (bf16[1024,256]{1,0:T(8,128)(2,1)S(1)}, bf16[1024,256]{1,0:T(8,128)(2,1)S(1)}, u32[]{:S(2)}, u32[]{:S(2)}) collective-permute-start(bf16[1024,256]{1,0:T(8,128)(2,1)S(1)} %copy-done.4), channel_id=1, source_target_pairs={{8,0},{40,8},{0,32},{32,40},{9,1},{41,9},{1,33},{33,41},{10,2},{42... | collective-permute-start | bytes 1572872 | tf_op jit(solution)/shard_map/ppermute | solution.py:429
  114.7 8.5 %collective-permute-start.27 = (bf16[512,256]{1,0:T(8,128)(2,1)S(1)}, bf16[512,256]{1,0:T(8,128)(2,1)S(1)}, u32[]{:S(2)}, u32[]{:S(2)}) collective-permute-start(bf16[512,256]{1,0:T(8,128)(2,1)S(1)} %collective-permute-done.26.refs_1_), channel_id=1, source_target_pairs={{0,1},{1,2},{2,3},{3,4},{4,5},{5,6},{6,7},{7,0},{8,9},{9,10},{10,1... | collective-permute-start | bytes 786440 | tf_op jit(solution)/shard_map/ppermute | solution.py:27
  114.7 8.5 %collective-permute-start.30 = (bf16[512,256]{1,0:T(8,128)(2,1)S(1)}, bf16[512,256]{1,0:T(8,128)(2,1)S(1)}, u32[]{:S(2)}, u32[]{:S(2)}) collective-permute-start(bf16[512,256]{1,0:T(8,128)(2,1)S(1)} %collective-permute-done.29.refs_6_), channel_id=1, source_target_pairs={{0,7},{1,0},{2,1},{3,2},{4,3},{5,4},{6,5},{7,6},{8,15},{9,8},{10,9... | collective-permute-start | bytes 786440 | tf_op jit(solution)/shard_map/ppermute | solution.py:27
  123.2 7.7 %collective-permute-start.28 = (bf16[512,256]{1,0:T(8,128)(2,1)S(1)}, bf16[512,256]{1,0:T(8,128)(2,1)S(1)}, u32[]{:S(2)}, u32[]{:S(2)}) collective-permute-start(bf16[512,256]{1,0:T(8,128)(2,1)S(1)} %collective-permute-done.27.refs_2_), channel_id=1, source_target_pairs={{0,1},{1,2},{2,3},{3,4},{4,5},{5,6},{6,7},{7,0},{8,9},{9,10},{10,1... | collective-permute-start | bytes 786440 | tf_op jit(solution)/shard_map/ppermute | solution.py:27
  123.2 7.7 %collective-permute-start.31 = (bf16[512,256]{1,0:T(8,128)(2,1)S(1)}, bf16[512,256]{1,0:T(8,128)(2,1)S(1)}, u32[]{:S(2)}, u32[]{:S(2)}) collective-permute-start(bf16[512,256]{1,0:T(8,128)(2,1)S(1)} %collective-permute-done.30.refs_5_), channel_id=1, source_target_pairs={{0,7},{1,0},{2,1},{3,2},{4,3},{5,4},{6,5},{7,6},{8,15},{9,8},{10,9... | collective-permute-start | bytes 786440 | tf_op jit(solution)/shard_map/ppermute | solution.py:27
  126.4 4.6 %collective-permute-start.34 = (bf16[1024,256]{1,0:T(8,128)(2,1)S(1)}, bf16[1024,256]{1,0:T(8,128)(2,1)S(1)}, u32[]{:S(2)}, u32[]{:S(2)}) collective-permute-start(bf16[1024,256]{1,0:T(8,128)(2,1)S(1)} %collective-permute-done.33.refs_7_.refs_1_), channel_id=1, source_target_pairs={{0,16},{16,0},{1,17},{17,1},{2,18},{18,2},{3,19},{19,3},{4,20},{20... | collective-permute-start | bytes 1572872 | tf_op jit(solution)/shard_map/ppermute | solution.py:439
  126.5 4.6 %collective-permute-start.36 = (bf16[1024,256]{1,0:T(8,128)(2,1)S(1)}, bf16[1024,256]{1,0:T(8,128)(2,1)S(1)}, u32[]{:S(2)}, u32[]{:S(2)}) collective-permute-start(bf16[1024,256]{1,0:T(8,128)(2,1)S(1)} %collective-permute-done.35.refs_9_.refs_3_), channel_id=1, source_target_pairs={{0,16},{16,0},{1,17},{17,1},{2,18},{18,2},{3,19},{19,3},{4,20},{20... | collective-permute-start | bytes 1572872 | tf_op jit(solution)/shard_map/ppermute | solution.py:439
  130.9 7.7 %collective-permute-start.32 = (bf16[512,256]{1,0:T(8,128)(2,1)S(1)}, bf16[512,256]{1,0:T(8,128)(2,1)S(1)}, u32[]{:S(2)}, u32[]{:S(2)}) collective-permute-start(bf16[512,256]{1,0:T(8,128)(2,1)S(1)} %broadcast_select_fusion), channel_id=1, source_target_pairs={{0,1},{1,2},{2,3},{3,4},{4,5},{5,6},{6,7},{7,0},{16,23},{17,16},{1... | collective-permute-start | bytes 786440 | tf_op jit(solution)/shard_map/ppermute | solution.py:38
  139.5 11.4 %collective-permute-start.37 = (bf16[512,256]{1,0:T(8,128)(2,1)S(1)}, bf16[512,256]{1,0:T(8,128)(2,1)S(1)}, u32[]{:S(2)}, u32[]{:S(2)}) collective-permute-start(bf16[512,256]{1,0:T(8,128)(2,1)S(1)} %get-tuple-element.38), channel_id=1, source_target_pairs={{0,8},{8,0},{1,9},{9,1},{2,10},{10,2},{3,11},{11,3},{4,12},{12,4},... | collective-permute-start | bytes 786440 | tf_op jit(solution)/shard_map/ppermute | solution.py:443
